TPU v7x, 32 devices: a whole 2x2x4 slice. The times are simulated.
32 devices in a mesh: dp: 8 (over z, y), seq: 4 (over x, core).
Axes of the slice: x: 2, y: 2, z: 4, core: 2. Of those that a mesh axis runs over, the one named last changes fastest.
Arguments:
- tokens: bfloat16 [8192, 768], P(('dp', 'seq')), may hold values from -6 to 6
- ln1_gain: bfloat16 [768], P('dp'), may hold values from 0.25 to 1.75
- w_qkv: bfloat16 [768, 2304], P('dp'), may hold values from -0.21875 to 0.21875
- w_out: bfloat16 [768, 768], P('dp'), may hold values from -1.75 to 1.75
- w_ada: bfloat16 [768, 2304], P('dp'), may hold values from -0.21875 to 0.21875
- w_up: bfloat16 [768, 3072], P('dp'), may hold values from -0.21875 to 0.21875
- w_down: bfloat16 [3072, 768], P('dp'), may hold values from -0.109375 to 0.109375
- out_grad: bfloat16 [8192, 768], P(('dp', 'seq')), may hold values from -6 to 6
- layout: int32 [8, 2], P('dp'), may hold values from 256 to 896, as said below
- timestep: int32 [8], P('dp'), may hold values from 0 to 999
Outputs:
- layer_out: bfloat16 [8192, 768], P(('dp', 'seq'))
- input_grad: bfloat16 [8192, 768], P(('dp', 'seq'))
- gain_grad: float32 [768], P('dp')
- qkv_weight_grad: float32 [768, 2304], P('dp')
- out_weight_grad: float32 [768, 768], P('dp')
- ada_weight_grad: float32 [768, 2304], P('dp')
- up_weight_grad: float32 [768, 3072], P('dp')
- down_weight_grad: float32 [3072, 768], P('dp')
Inputs may be any that keep to these rules, and one draw needn't show every extreme that they name: layout[g] = (P, C): tokens below P are the prompt, the first continuation runs from P to C - 1, the second from C to 1023; P lies between 256 and 512, and each continuation holds at least a quarter of the tokens after the prompt.
All inputs are finite; a program needn't handle non-finite values.
Results may differ from a plain program's by a relative error of at most 0.017.
Values may be sent and summed in bfloat16 or wider, within the bound.
No kernel may reach another device: no remote copies, remote signals or barrier semaphores. Data moves between devices by JAX's collectives and lax.ppermute only.
A program may use at most 128 MiB of HBM per device.

v0:
```python
import math

import jax
import jax.numpy as jnp
from jax import lax
from jax.sharding import PartitionSpec as P

HEADS = 12
HEAD_DIM = 64


eps = 1e-05
neg_fill = -1e30


def layer_norm(values_in):
    average = jnp.mean(values_in, axis=-1, keepdims=True)
    centred = values_in - average
    variance = jnp.mean(centred * centred, axis=-1, keepdims=True)
    scaling = lax.rsqrt(variance + eps)
    return (centred * scaling, scaling)


def norm_back(grad_normed, normed, scaling):
    first_mean = jnp.mean(grad_normed, axis=-1, keepdims=True)
    second_mean = jnp.mean(grad_normed * normed, axis=-1, keepdims=True)
    return scaling * (grad_normed - first_mean - normed * second_mean)


def rope_tables(positions):
    half_dim = HEAD_DIM // 2
    frequency = jnp.exp(
        -math.log(10000.0) * 2.0 * jnp.arange(half_dim, dtype=jnp.float32) / HEAD_DIM
    )
    angles = positions.astype(jnp.float32)[:, None] * frequency[None, :]
    return (jnp.cos(angles), jnp.sin(angles))


def rotate(values_in, cos_table, sine_table, direction):
    half_dim = HEAD_DIM // 2
    front_half = values_in[..., :half_dim]
    back_half = values_in[..., half_dim:]
    cos_part = cos_table[:, None, :]
    sine_part = sine_table[:, None, :] * direction
    return jnp.concatenate(
        [
            front_half * cos_part - back_half * sine_part,
            back_half * cos_part + front_half * sine_part,
        ],
        axis=-1,
    )


def visible(query_pos, key_pos, prompt_end, second_start):
    query_segment = (query_pos >= prompt_end).astype(jnp.int32) + (
        query_pos >= second_start
    ).astype(jnp.int32)
    key_segment = (key_pos >= prompt_end).astype(jnp.int32) + (key_pos >= second_start).astype(
        jnp.int32
    )
    return (key_pos[None, :] < prompt_end) | (query_segment[:, None] == key_segment[None, :])


def time_table(time_steps, model_width):
    half_dim = model_width // 2
    frequency = jnp.exp(-math.log(10000.0) * jnp.arange(half_dim, dtype=jnp.float32) / half_dim)
    angles = time_steps[:, None] * frequency[None, :]
    return jnp.concatenate([jnp.cos(angles), jnp.sin(angles)], axis=1)


def left_product(left, right):
    return lax.dot_general(
        left, right, (((0,), (0,)), ((), ())), preferred_element_type=jnp.float32
    )


def right_product(left, right):
    return lax.dot_general(
        left, right, (((1,), (1,)), ((), ())), preferred_element_type=jnp.float32
    )


def split_rows(grad_full, data_count):
    return grad_full.reshape(data_count, grad_full.shape[0] // data_count, -1)


def body(tokens, ln1_gain, w_qkv, w_out, w_ada, w_up, w_down, out_grad, layout, timestep):
    seq_count = lax.axis_size("seq")
    seq_rank = lax.axis_index("seq")
    tok_rows = tokens.shape[0]
    model_width = tokens.shape[1]
    group_rows = tok_rows * seq_count
    heads_local = HEADS // seq_count
    local_width = heads_local * HEAD_DIM
    block_rows = min(512, group_rows)
    blocks = group_rows // block_rows
    gain_full, qkv_weight, out_weight = (
        lax.all_gather(ln1_gain, "dp", axis=0, tiled=True),
        lax.all_gather(w_qkv, "dp", axis=0, tiled=True),
        lax.all_gather(w_out, "dp", axis=0, tiled=True),
    )
    ada_weight, up_weight, down_weight = (
        lax.all_gather(w_ada, "dp", axis=0, tiled=True),
        lax.all_gather(w_up, "dp", axis=0, tiled=True),
        lax.all_gather(w_down, "dp", axis=0, tiled=True),
    )
    gain_float = gain_full.astype(jnp.float32)
    inputs = tokens.astype(jnp.float32)
    normed_one, scaling_one = layer_norm(inputs)
    hidden_one = (normed_one * gain_float).astype(jnp.bfloat16)
    projected = jnp.dot(hidden_one, qkv_weight, preferred_element_type=jnp.float32).reshape(
        tok_rows, 3, HEADS, HEAD_DIM
    )
    positions = seq_rank * tok_rows + jnp.arange(tok_rows, dtype=jnp.int32)
    cos_table, sine_table = rope_tables(positions)
    rotated = jnp.stack(
        [
            rotate(projected[:, 0], cos_table, sine_table, 1.0),
            rotate(projected[:, 1], cos_table, sine_table, 1.0),
            projected[:, 2],
        ],
        axis=1,
    )
    outgoing = rotated.astype(jnp.bfloat16).reshape(tok_rows, 3, seq_count, local_width)
    incoming = lax.all_to_all(outgoing, "seq", split_axis=2, concat_axis=0, tiled=True).reshape(
        group_rows, 3, heads_local, HEAD_DIM
    )
    queries = incoming[:, 0]
    keys_all = incoming[:, 1]
    values_all = incoming[:, 2]
    prompt_end = layout[0, 0]
    second_start = layout[0, 1]
    key_pos = jnp.arange(group_rows, dtype=jnp.int32)

    def scores_of(query_block, start):
        raw_scores = (
            jnp.einsum("qhd,khd->hqk", query_block, keys_all, preferred_element_type=jnp.float32)
            * 0.125
        )
        query_pos = start + jnp.arange(block_rows, dtype=jnp.int32)
        allowed = visible(query_pos, key_pos, prompt_end, second_start)
        return jnp.where(allowed[None], raw_scores, neg_fill)

    query_blocks = queries.reshape(blocks, block_rows, heads_local, HEAD_DIM)
    starts = jnp.arange(blocks, dtype=jnp.int32) * block_rows

    def forward_block(operands):
        query_block, start = operands
        scores = scores_of(query_block, start)
        row_max = jnp.max(scores, axis=-1, keepdims=True)
        exponent = jnp.exp(scores - row_max)
        row_sum = jnp.sum(exponent, axis=-1, keepdims=True)
        attn_probs = (exponent / row_sum).astype(jnp.bfloat16)
        block_out = jnp.einsum(
            "hqk,khd->qhd", attn_probs, values_all, preferred_element_type=jnp.float32
        )
        return (block_out.astype(jnp.bfloat16), (row_max + jnp.log(row_sum))[..., 0])

    attended_heads, log_sums = lax.map(forward_block, (query_blocks, starts))
    attended = lax.all_to_all(
        attended_heads.reshape(group_rows, local_width),
        "seq",
        split_axis=0,
        concat_axis=1,
        tiled=True,
    )
    middle = inputs + jnp.dot(attended, out_weight, preferred_element_type=jnp.float32)
    time_embed = time_table(timestep.astype(jnp.float32), model_width).astype(jnp.bfloat16)
    modulation = jnp.dot(time_embed, ada_weight, preferred_element_type=jnp.float32)[0]
    mod_scale = modulation[:model_width]
    mod_shift = modulation[model_width : 2 * model_width]
    mod_gate = modulation[2 * model_width :]
    normed_two, scaling_two = layer_norm(middle)
    hidden_two = (normed_two * (1.0 + mod_scale) + mod_shift).astype(jnp.bfloat16)
    pre_act = jnp.dot(hidden_two, up_weight, preferred_element_type=jnp.float32)
    gelu_vals, gelu_pull = jax.vjp(lambda inner: jax.nn.gelu(inner, approximate=True), pre_act)
    activated = gelu_vals.astype(jnp.bfloat16)
    mlp_out = jnp.dot(activated, down_weight, preferred_element_type=jnp.float32)
    result = middle + mod_gate * mlp_out
    grad_out = out_grad.astype(jnp.float32)
    grad_mlp = (mod_gate * grad_out).astype(jnp.bfloat16)
    grad_gate = jnp.sum(grad_out * mlp_out, axis=0)
    grad_wdown = left_product(activated, grad_mlp)
    grad_act = right_product(grad_mlp, down_weight)
    grad_pre = gelu_pull(grad_act)[0].astype(jnp.bfloat16)
    grad_wup = left_product(hidden_two, grad_pre)
    grad_hidden_two = right_product(grad_pre, up_weight)
    grad_scale = jnp.sum(grad_hidden_two * normed_two, axis=0)
    grad_shift = jnp.sum(grad_hidden_two, axis=0)
    grad_middle = grad_out + norm_back(grad_hidden_two * (1.0 + mod_scale), normed_two, scaling_two)
    grad_mod = jnp.concatenate([grad_scale, grad_shift, grad_gate])
    grad_branch = grad_middle.astype(jnp.bfloat16)
    grad_wout = left_product(attended, grad_branch)
    grad_attn = right_product(grad_branch, out_weight).astype(jnp.bfloat16)
    grad_heads = lax.all_to_all(grad_attn, "seq", split_axis=1, concat_axis=0, tiled=True).reshape(
        blocks, block_rows, heads_local, HEAD_DIM
    )

    def backward_block(carry, operands):
        key_grad, value_grad = carry
        query_block, start, grad_block, lse_block = operands
        scores = scores_of(query_block, start)
        attn_probs = jnp.exp(scores - lse_block[..., None])
        value_grad = value_grad + jnp.einsum(
            "hqk,qhd->khd",
            attn_probs.astype(jnp.bfloat16),
            grad_block,
            preferred_element_type=jnp.float32,
        )
        prob_grad = jnp.einsum(
            "qhd,khd->hqk", grad_block, values_all, preferred_element_type=jnp.float32
        )
        row_centre = jnp.sum(attn_probs * prob_grad, axis=-1, keepdims=True)
        score_grad = (attn_probs * (prob_grad - row_centre)).astype(jnp.bfloat16)
        query_grad = (
            jnp.einsum("hqk,khd->qhd", score_grad, keys_all, preferred_element_type=jnp.float32)
            * 0.125
        )
        key_grad = (
            key_grad
            + jnp.einsum(
                "hqk,qhd->khd", score_grad, query_block, preferred_element_type=jnp.float32
            )
            * 0.125
        )
        return ((key_grad, value_grad), query_grad)

    zero_grad = jnp.zeros((group_rows, heads_local, HEAD_DIM), jnp.float32)
    (key_grad, value_grad), query_grads = lax.scan(
        backward_block, (zero_grad, zero_grad), (query_blocks, starts, grad_heads, log_sums)
    )
    stacked = jnp.stack(
        [query_grads.reshape(group_rows, heads_local, HEAD_DIM), key_grad, value_grad], axis=1
    )
    stacked = stacked.astype(jnp.bfloat16).reshape(group_rows, 3, 1, local_width)
    returned = (
        lax.all_to_all(stacked, "seq", split_axis=0, concat_axis=2, tiled=True)
        .astype(jnp.float32)
        .reshape(tok_rows, 3, HEADS, HEAD_DIM)
    )
    grad_qkv = jnp.stack(
        [
            rotate(returned[:, 0], cos_table, sine_table, -1.0),
            rotate(returned[:, 1], cos_table, sine_table, -1.0),
            returned[:, 2],
        ],
        axis=1,
    )
    grad_qkv = grad_qkv.reshape(tok_rows, 3 * model_width).astype(jnp.bfloat16)
    grad_wqkv = left_product(hidden_one, grad_qkv)
    grad_hidden_one = right_product(grad_qkv, qkv_weight)
    grad_gain = jnp.sum(grad_hidden_one * normed_one, axis=0)
    grad_inputs = grad_middle + norm_back(grad_hidden_one * gain_float, normed_one, scaling_one)
    qkv_cols = 3 * model_width
    grad_wada = time_embed.astype(jnp.float32).reshape(-1)[:, None] * grad_mod[None, :]
    grad_joint = jnp.concatenate([grad_wqkv, grad_wada], axis=1)
    data_count = lax.axis_size("dp")
    parts = (
        lax.psum_scatter(
            split_rows(grad_gain, data_count).astype(jnp.bfloat16),
            "seq",
            scatter_dimension=1,
            tiled=True,
        ).astype(jnp.float32),
        lax.psum_scatter(
            split_rows(grad_joint, data_count).astype(jnp.bfloat16),
            "seq",
            scatter_dimension=1,
            tiled=True,
        ).astype(jnp.float32),
        lax.psum_scatter(
            split_rows(grad_wout, data_count).astype(jnp.bfloat16),
            "seq",
            scatter_dimension=1,
            tiled=True,
        ).astype(jnp.float32),
        lax.psum_scatter(
            split_rows(grad_wup, data_count).astype(jnp.bfloat16),
            "seq",
            scatter_dimension=1,
            tiled=True,
        ).astype(jnp.float32),
        lax.psum_scatter(
            split_rows(grad_wdown, data_count).astype(jnp.bfloat16),
            "seq",
            scatter_dimension=1,
            tiled=True,
        ).astype(jnp.float32),
    )
    owned = (
        lax.psum_scatter(parts[0], "dp", scatter_dimension=0, tiled=True),
        lax.psum_scatter(parts[1], "dp", scatter_dimension=0, tiled=True),
        lax.psum_scatter(parts[2], "dp", scatter_dimension=0, tiled=True),
        lax.psum_scatter(parts[3], "dp", scatter_dimension=0, tiled=True),
        lax.psum_scatter(parts[4], "dp", scatter_dimension=0, tiled=True),
    )
    spread = (
        lax.all_gather(owned[0].astype(jnp.bfloat16), "seq", axis=1, tiled=True).astype(
            jnp.float32
        ),
        lax.all_gather(owned[1].astype(jnp.bfloat16), "seq", axis=1, tiled=True).astype(
            jnp.float32
        ),
        lax.all_gather(owned[2].astype(jnp.bfloat16), "seq", axis=1, tiled=True).astype(
            jnp.float32
        ),
        lax.all_gather(owned[3].astype(jnp.bfloat16), "seq", axis=1, tiled=True).astype(
            jnp.float32
        ),
        lax.all_gather(owned[4].astype(jnp.bfloat16), "seq", axis=1, tiled=True).astype(
            jnp.float32
        ),
    )
    final_gain = spread[0].reshape(-1)
    final_joint = spread[1].reshape(spread[1].shape[1], -1)
    final_out = spread[2].reshape(spread[2].shape[1], -1)
    final_up = spread[3].reshape(spread[3].shape[1], -1)
    final_down = spread[4].reshape(spread[4].shape[1], -1)
    final_qkv = final_joint[:, :qkv_cols]
    final_ada = final_joint[:, qkv_cols:]
    return (
        result.astype(jnp.bfloat16),
        grad_inputs.astype(jnp.bfloat16),
        final_gain,
        final_qkv,
        final_out,
        final_ada,
        final_up,
        final_down,
    )


def solution(mesh):
    placed = (
        P(("dp", "seq"), None),
        P("dp"),
        P("dp", None),
        P("dp", None),
        P("dp", None),
        P("dp", None),
        P("dp", None),
        P(("dp", "seq"), None),
        P("dp", None),
        P("dp"),
    )
    return jax.shard_map(
        body,
        mesh=mesh,
        in_specs=placed,
        out_specs=(
            P(("dp", "seq"), None),
            P(("dp", "seq"), None),
            P("dp"),
            P("dp", None),
            P("dp", None),
            P("dp", None),
            P("dp", None),
            P("dp", None),
        ),
        check_vma=False,
    )
```

profile of v0, /device:TPU:0, one launch (start us, length us, event | category | flops | bytes accessed | tf_op | source)
XLA Modules:
  0.0 863.7 jit_solution(9710499089409813553)
XLA Ops:
  12.9 23.2 %all-reduce = bf16[768]{0:T(1024)(128)(2,1)S(1)} all-reduce(bf16[768]{0:T(1024)(128)(2,1)S(1)} %dynamic-update-slice), channel_id=1, replica_groups=mesh['dp'=8,'seq'=4] {'dp'}, use_global_device_ids=true, to_apply=%add | all-reduce | flops 768 | bytes 3072
  39.3 39.0 %all-gather.6.cloned.1.call-done = bf16[768,2304]{1,0:T(8,128)(2,1)} async-done(((bf16[96,2304]{1,0:T(8,128)(2,1)}), bf16[768,2304]{1,0:T(8,128)(2,1)}) %all-gather.6.cloned.1.call-update) | async-done | bytes 3538960 | tf_op jit(solution)/shard_map/all_gather | solution.py:99
  89.9 13.3 %all-to-all-done = bf16[256,3,4,192]{0,3,1,2:T(8,128)(2,1)S(1)} async-done(((bf16[256,3,4,192]{0,3,1,2:T(8,128)(2,1)}), bf16[256,3,4,192]{0,3,1,2:T(8,128)(2,1)S(1)}, u32[]{:S(2)}, u32[]{:S(2)}) %all-to-all-start) | async-done | bytes 1179680 | tf_op jit(solution)/shard_map/all_to_all | solution.py:125
  106.9 25.5 %while.30 = (s32[]{:T(128)}, bf16[2,512,3,64]{1,3,2,0:T(8,128)(2,1)S(1)}, f32[2,3,512]{2,1,0:T(4,128)}, s32[]{:T(128)}, s32[2]{0:T(128)S(1)}, /*index=5*/s32[]{:...) while((s32[]{:T(128)}, ...), condition=%wide.region_5.6_spmd.clone.clone, body=%wide.region_2.5_spmd.clone.clone.sunk | while | flops 422682112 | bytes 22220956 | solution.py:159
  137.5 6.7 all-gather.10.cloned.1.call-done
  146.8 39.1 %all-gather.8.cloned.1.call-done = bf16[768,768]{1,0:T(8,128)(2,1)} async-done(((bf16[96,768]{1,0:T(8,128)(2,1)}), bf16[768,768]{1,0:T(8,128)(2,1)}) %all-gather.8.cloned.1.call-update) | async-done | bytes 1179664 | tf_op jit(solution)/shard_map/all_gather | solution.py:100
  188.1 78.6 %all-gather.12.cloned.1.call-done = bf16[768,3072]{1,0:T(8,128)(2,1)} async-done(((bf16[96,3072]{1,0:T(8,128)(2,1)}), bf16[768,3072]{1,0:T(8,128)(2,1)}) %all-gather.12.cloned.1.call-update) | async-done | bytes 4718608 | tf_op jit(solution)/shard_map/all_gather | solution.py:104
  266.7 5.5 fusion.87
  272.2 74.6 %all-gather.14.cloned.1.call-done = bf16[3072,768]{1,0:T(8,128)(2,1)} async-done(((bf16[384,768]{1,0:T(8,128)(2,1)}), bf16[3072,768]{1,0:T(8,128)(2,1)}) %all-gather.14.cloned.1.call-update) | async-done | bytes 4718608 | tf_op jit(solution)/shard_map/all_gather | solution.py:105
  346.8 6.7 fusion.56
  362.6 6.4 convolution_convert_fusion
  381.0 5.4 all-to-all-done.2
  387.7 45.0 %while.31 = (s32[]{:T(128)}, f32[1024,3,64]{0,2,1:T(8,128)}, f32[1024,3,64]{0,2,1:T(8,128)}, bf16[2,512,3,64]{1,3,2,0:T(8,128)(2,1)}, bf16[2,512,3,64]{1,3,2,0:T...) while((s32[]{:T(128)}, f32[1024,3,64]{0,2,1:T(8,128)}, ...), condition=%wide.region_12.13_spmd.clone.clone, body=%wide.region_10.12_spmd.clone.clone.sunk | while | flops 1032363520 | bytes 110420320 | solution.py:229
  395.2 3.8 multiply_reduce_fusion.7
  404.1 4.0 fusion.155
  417.4 3.8 multiply_reduce_fusion.7
  426.6 4.3 fusion.155
  445.6 30.8 %all-to-all-done.3 = bf16[1024,3,1,192]{3,1,2,0:T(4,128)(2,1)S(1)} async-done(((bf16[1024,3,1,192]{3,1,2,0:T(4,128)(2,1)}), bf16[1024,3,1,192]{3,1,2,0:T(4,128)(2,1)S(1)}, u32[]{:S(2)}, u32[]{:S(2)}) %all-to-all-start.3) | async-done | bytes 1179680 | tf_op jit(solution)/shard_map/all_to_all | solution.py:237
  482.5 5.5 pad_maximum_fusion
  488.0 6.7 copy.95
  501.7 56.8 %reduce-scatter.27.cloned.1.call-done = bf16[24,36864]{1,0:T(8,128)(2,1)} async-done(((bf16[96,36864]{1,0:T(8,128)(2,1)}), bf16[24,36864]{1,0:T(8,128)(2,1)}) %reduce-scatter.27.cloned.1.call-update) | async-done | bytes 1769488
  567.7 5.7 all-reduce.2
  573.5 21.7 %all-reduce.3 = bf16[8,24,1]{1,0,2:T(8,128)(2,1)S(1)} all-reduce(f32[8,24,1]{1,0,2:T(8,128)S(1)} %dynamic-slice_convert_fusion), channel_id=3, replica_groups=mesh['dp'=8,'seq'=4] {'dp'}, use_global_device_ids=true, to_apply=%region_17.18.clone | all-reduce | flops 192 | bytes 1152
  596.1 5.6 all-reduce.1
  603.3 21.1 %reduce-scatter.19.cloned.1.call-done = f32[1,24,768]{2,1,0:T(8,128)} async-done(((f32[8,24,768]{2,1,0:T(8,128)}), f32[1,24,768]{2,1,0:T(8,128)}) %reduce-scatter.19.cloned.1.call-update) | async-done | bytes 73744 | tf_op jit(solution)/shard_map/reduce_scatter | solution.py:293
  625.3 5.5 all_gather.41
  631.4 59.9 %reduce-scatter.25.cloned.1.call-done = bf16[1,96,768]{2,1,0:T(8,128)(2,1)} async-done(((bf16[8,96,768]{2,1,0:T(8,128)(2,1)}), bf16[1,96,768]{2,1,0:T(8,128)(2,1)}) %reduce-scatter.25.cloned.1.call-update) | async-done | bytes 147472 | tf_op jit(solution)/shard_map/reduce_scatter | solution.py:295
  691.4 7.7 all_gather.43
  700.2 62.9 %reduce-scatter.21.cloned.1.call-done = f32[1,24,3072]{2,1,0:T(8,128)} async-done(((f32[8,24,3072]{2,1,0:T(8,128)}), f32[1,24,3072]{2,1,0:T(8,128)}) %reduce-scatter.21.cloned.1.call-update) | async-done | bytes 294928 | tf_op jit(solution)/shard_map/reduce_scatter | solution.py:294
  764.1 7.5 all_gather.42
  772.8 72.5 %reduce-scatter.17.cloned.1.call-done = f32[1,24,4608]{2,1,0:T(8,128)} async-done(((f32[8,24,4608]{2,1,0:T(8,128)}), f32[1,24,4608]{2,1,0:T(8,128)}) %reduce-scatter.17.cloned.1.call-update) | async-done | bytes 442384 | tf_op jit(solution)/shard_map/reduce_scatter | solution.py:292
  846.2 9.1 %all_gather.40 = bf16[1,96,4608]{2,1,0:T(8,128)(2,1)S(1)} all-gather(bf16[1,24,4608]{2,1,0:T(8,128)(2,1)S(1)} %convert_element_type.256), channel_id=1, replica_groups=mesh['dp'=8,'seq'=4] {'seq'}, dimensions={1}, use_global_device_ids=true | all-gather | bytes 1105920 | tf_op jit(solution)/shard_map/all_gather | solution.py:301
  (242 shorter events, 152.6 us)
Async XLA Ops:
  7.2 71.1 %all-gather.6.cloned.1.call-start = ((), (), s32[]{:S(2)}) async-start(), calls=%async_computation.12 | async-start | bytes 3981312 | tf_op jit(solution)/shard_map/all_gather | solution.py:99
  7.9 136.3 %all-gather.10.cloned.1.call-start = ((), (), s32[]{:S(2)}) async-start(), calls=%async_computation.14 | async-start | bytes 3981312 | tf_op jit(solution)/shard_map/all_gather | solution.py:103
  8.6 177.3 %all-gather.8.cloned.1.call-start = ((), (), s32[]{:S(2)}) async-start(), calls=%async_computation.13 | async-start | bytes 1327104 | tf_op jit(solution)/shard_map/all_gather | solution.py:100
  9.4 257.3 %all-gather.12.cloned.1.call-start = ((), (), s32[]{:S(2)}) async-start(), calls=%async_computation.15 | async-start | bytes 5308416 | tf_op jit(solution)/shard_map/all_gather | solution.py:104
  36.1 46.0 %copy-start.13 = (f32[768]{0:T(1024)}, f32[768]{0:T(1024)S(1)}, u32[]{:S(2)}) copy-start(f32[768]{0:T(1024)S(1)} %convert_element_type.231) | copy-start | bytes 9220
  37.2 44.8 %copy-start.16 = (f32[256]{0:T(256)}, f32[256]{0:T(256)S(1)}, u32[]{:S(2)}) copy-start(f32[256]{0:T(256)S(1)} %broadcast_multiply_fusion.6) | copy-start | bytes 3076
  38.5 43.6 %copy-start.18 = (f32[256]{0:T(256)}, f32[256]{0:T(256)S(1)}, u32[]{:S(2)}) copy-start(f32[256]{0:T(256)S(1)} %add_rsqrt_fusion.1) | copy-start | bytes 3076
  39.3 42.9 %copy-start.11 = (f32[256,32]{0,1:T(8,128)}, f32[256,32]{0,1:T(8,128)S(1)}, u32[]{:S(2)}) copy-start(f32[256,32]{0,1:T(8,128)S(1)} %get-tuple-element.453) | copy-start | bytes 98308
  82.7 6.6 copy-start.24
  83.8 19.4 %all-to-all-start = ((bf16[256,3,4,192]{0,3,1,2:T(8,128)(2,1)}), bf16[256,3,4,192]{0,3,1,2:T(8,128)(2,1)S(1)}, u32[]{:S(2)}, u32[]{:S(2)}) async-start(bf16[256,3,4,192]{0,3,1,2:T(8,128)(2,1)} %copy.70), calls=%async_computation | async-start | bytes 2359296 | tf_op jit(solution)/shard_map/all_to_all | solution.py:125
  87.4 259.4 %all-gather.14.cloned.1.call-start = ((), (), s32[]{:S(2)}) async-start(), calls=%async_computation.16 | async-start | bytes 5308416 | tf_op jit(solution)/shard_map/all_gather | solution.py:105
  132.4 14.4 %copy-start.28 = (s32[2]{0:T(128)}, s32[2]{0:T(128)S(1)}, u32[]{:S(2)}) copy-start(s32[2]{0:T(128)S(1)} %get-tuple-element.735) | copy-start | bytes 28
  132.8 53.1 %copy-start.3 = (bf16[256,768]{1,0:T(8,128)(2,1)S(1)}, bf16[256,768]{1,0:T(8,128)(2,1)}, u32[]{:S(2)}) copy-start(bf16[256,768]{1,0:T(8,128)(2,1)} %param.14) | copy-start | bytes 1179652
  133.8 52.2 %all-to-all-start.1 = ((bf16[4,256,192]{1,2,0:T(8,128)(2,1)}), bf16[4,256,192]{1,2,0:T(8,128)(2,1)S(1)}, u32[]{:S(2)}, u32[]{:S(2)}) async-start(bf16[4,256,192]{1,2,0:T(8,128)(2,1)} %copy.74), calls=%async_computation.1 | async-start | bytes 786432 | tf_op jit(solution)/shard_map/all_to_all | solution.py:160
  137.3 357.5 %reduce-scatter.29.cloned.1.call-start = ((), (), s32[]{:S(2)}) async-start(), calls=%async_computation.23 | async-start | bytes 1474560
  266.7 80.1 %copy-start.27 = (bf16[256,768]{1,0:T(8,128)(2,1)S(1)}, bf16[256,768]{1,0:T(8,128)(2,1)}, u32[]{:S(2)}) copy-start(bf16[256,768]{1,0:T(8,128)(2,1)} %param.21) | copy-start | bytes 1179652
  346.8 6.8 copy-start.25
  360.9 8.1 copy-start.5
  362.5 134.3 %reduce-scatter.23.cloned.1.call-start = ((), (), s32[]{:S(2)}) async-start(), calls=%async_computation.20 | async-start | bytes 5898240 | tf_op jit(solution)/shard_map/reduce_scatter | solution.py:283
  371.7 14.7 %all-to-all-start.2 = ((bf16[256,4,192]{0,2,1:T(8,128)(2,1)}), bf16[256,4,192]{0,2,1:T(8,128)(2,1)S(1)}, u32[]{:S(2)}, u32[]{:S(2)}) async-start(bf16[256,4,192]{0,2,1:T(8,128)(2,1)} %bitcast.16), calls=%async_computation.2 | async-start | bytes 786432 | tf_op jit(solution)/shard_map/all_to_all | solution.py:195
  375.1 122.4 %reduce-scatter.31.cloned.1.call-start = ((), (), s32[]{:S(2)}) async-start(), calls=%async_computation.24 | async-start | bytes 5898240
  381.0 6.7 copy-start.29
  389.7 9.3 %copy-start = (f32[3,512,1024]{2,1,0:T(8,128)}, f32[3,512,1024]{2,1,0:T(8,128)S(1)}, u32[]{:S(2)}) copy-start(f32[3,512,1024]{2,1,0:T(8,128)S(1)} %fusion.153) | copy-start | bytes 18874372 | tf_op jit(solution)/shard_map/while
  412.0 9.2 %copy-start = (f32[3,512,1024]{2,1,0:T(8,128)}, f32[3,512,1024]{2,1,0:T(8,128)S(1)}, u32[]{:S(2)}) copy-start(f32[3,512,1024]{2,1,0:T(8,128)S(1)} %fusion.153) | copy-start | bytes 18874372 | tf_op jit(solution)/shard_map/while
  436.9 6.5 copy-start.20
  439.5 37.0 %all-to-all-start.3 = ((bf16[1024,3,1,192]{3,1,2,0:T(4,128)(2,1)}), bf16[1024,3,1,192]{3,1,2,0:T(4,128)(2,1)S(1)}, u32[]{:S(2)}, u32[]{:S(2)}) async-start(bf16[1024,3,1,192]{3,1,2,0:T(4,128)(2,1)} %copy.80), calls=%async_computation.3 | async-start | bytes 4194304 | tf_op jit(solution)/shard_map/all_to_all | solution.py:237
  443.1 115.4 %reduce-scatter.27.cloned.1.call-start = ((), (), s32[]{:S(2)}) async-start(), calls=%async_computation.22 | async-start | bytes 8847360
  494.7 129.7 %reduce-scatter.19.cloned.1.call-start = ((), (), s32[]{:S(2)}) async-start(), calls=%async_computation.18 | async-start | bytes 663552 | tf_op jit(solution)/shard_map/reduce_scatter | solution.py:293
  496.7 194.7 %reduce-scatter.25.cloned.1.call-start = ((), (), s32[]{:S(2)}) async-start(), calls=%async_computation.21 | async-start | bytes 1327104 | tf_op jit(solution)/shard_map/reduce_scatter | solution.py:295
  497.5 265.7 %reduce-scatter.21.cloned.1.call-start = ((), (), s32[]{:S(2)}) async-start(), calls=%async_computation.19 | async-start | bytes 2654208 | tf_op jit(solution)/shard_map/reduce_scatter | solution.py:294
  501.6 343.6 %reduce-scatter.17.cloned.1.call-start = ((), (), s32[]{:S(2)}) async-start(), calls=%async_computation.17 | async-start | bytes 3981312 | tf_op jit(solution)/shard_map/reduce_scatter | solution.py:292
  564.2 38.0 %copy-start.6 = (f32[256,768]{1,0:T(8,128)S(1)}, f32[256,768]{1,0:T(8,128)}, u32[]{:S(2)}) copy-start(f32[256,768]{1,0:T(8,128)} %copy-done.5) | copy-start | bytes 2359300
  (21 other events, 59.5 us)
Sparse Core Ops, SparseCore 0:
  10.2 68.0 all-gather.5
  80.5 63.6 all-gather.9
  146.4 39.5 all-gather.7
  188.0 78.6 all-gather.11
  268.7 78.0 all-gather.13
  362.6 27.1 reduce-scatter.28
  392.5 45.1 reduce-scatter.22
  440.3 55.2 reduce-scatter.30
  498.2 60.2 reduce-scatter.26
  562.2 62.1 reduce-scatter.18
  628.1 63.1 reduce-scatter.24
  695.1 67.9 reduce-scatter.20
  767.2 77.9 reduce-scatter.16
where the time goes:
time: 873 us; the launch traced here: 864 us
  waiting for transfers between devices  565 us (65%)
  blocking collectives  86 us (10%)
  matrix products  79.6 us (9%)
  other arithmetic  53.6 us (6%)
  local copies, waits for them, and re-layouts  46.8 us (5%)
  between operations  17.5 us (2%)
  starting transfers between devices  15.2 us (2%)
    all_gather x1, waiting for transfers between devices, body(): lax.all_gather(w_up, 'dp', axis=0, tiled=True)  78.6 us
    all_gather x1, waiting for transfers between devices, body(): lax.all_gather(w_down, 'dp', axis=0, tiled=True)  74.6 us
    reduce_scatter x1, waiting for transfers between devices, body(): lax.psum_scatter(parts[1], 'dp', scatter_dimension=0, tiled=True)  72.5 us
    reduce_scatter x1, waiting for transfers between devices, body(): lax.psum_scatter(parts[3], 'dp', scatter_dimension=0, tiled=True)  62.9 us
    unnamed x16, waiting for transfers between devices  60.7 us
    reduce_scatter x1, waiting for transfers between devices, body(): lax.psum_scatter(parts[4], 'dp', scatter_dimension=0, tiled=True)  59.9 us
    unnamed x4, blocking collectives  56.2 us
    all_gather x1, waiting for transfers between devices, body(): lax.all_gather(w_out, 'dp', axis=0, tiled=True)  39.1 us
  transfers between devices with their start and end apart: 17, of which 13 were waited for; matrix products, arithmetic and copies ran while one was open for 18% of the time, Pallas kernels for 0%

commit v1 on v0

v1 whole, which is shorter than its diff:
```python
import math

import jax
import jax.numpy as jnp
from jax import lax
from jax.sharding import PartitionSpec as P

HEADS = 12
HEAD_DIM = 64

eps = 1e-05
neg_fill = -1e30

MASKS = (0, 2, 1, 3)


def layer_norm(values_in):
    average = jnp.mean(values_in, axis=-1, keepdims=True)
    centred = values_in - average
    variance = jnp.mean(centred * centred, axis=-1, keepdims=True)
    scaling = lax.rsqrt(variance + eps)
    return (centred * scaling, scaling)


def norm_back(grad_normed, normed, scaling):
    first_mean = jnp.mean(grad_normed, axis=-1, keepdims=True)
    second_mean = jnp.mean(grad_normed * normed, axis=-1, keepdims=True)
    return scaling * (grad_normed - first_mean - normed * second_mean)


def rope_tables(positions):
    half_dim = HEAD_DIM // 2
    frequency = jnp.exp(
        -math.log(10000.0) * 2.0 * jnp.arange(half_dim, dtype=jnp.float32) / HEAD_DIM
    )
    angles = positions.astype(jnp.float32)[:, None] * frequency[None, :]
    return (jnp.cos(angles), jnp.sin(angles))


def rotate(values_in, cos_table, sine_table, direction):
    half_dim = HEAD_DIM // 2
    front_half = values_in[..., :half_dim]
    back_half = values_in[..., half_dim:]
    cos_part = cos_table[:, None, :]
    sine_part = sine_table[:, None, :] * direction
    return jnp.concatenate(
        [
            front_half * cos_part - back_half * sine_part,
            back_half * cos_part + front_half * sine_part,
        ],
        axis=-1,
    )


def visible(query_pos, key_pos, prompt_end, second_start):
    query_segment = (query_pos >= prompt_end).astype(jnp.int32) + (
        query_pos >= second_start
    ).astype(jnp.int32)
    key_segment = (key_pos >= prompt_end).astype(jnp.int32) + (key_pos >= second_start).astype(
        jnp.int32
    )
    return (key_pos[None, :] < prompt_end) | (query_segment[:, None] == key_segment[None, :])


def time_table(time_steps, model_width):
    half_dim = model_width // 2
    frequency = jnp.exp(-math.log(10000.0) * jnp.arange(half_dim, dtype=jnp.float32) / half_dim)
    angles = time_steps[:, None] * frequency[None, :]
    return jnp.concatenate([jnp.cos(angles), jnp.sin(angles)], axis=1)


def left_product(left, right):
    return lax.dot_general(
        left, right, (((0,), (0,)), ((), ())), preferred_element_type=jnp.float32
    )


def right_product(left, right):
    return lax.dot_general(
        left, right, (((1,), (1,)), ((), ())), preferred_element_type=jnp.float32
    )


def low(values_in):
    return values_in.astype(jnp.bfloat16)


def wide(values_in):
    return values_in.astype(jnp.float32)


def hop(values_in, mask):
    return lax.ppermute(values_in, "seq", [(i, i ^ mask) for i in range(lax.axis_size("seq"))])


def spread(values_in):
    beside = jnp.concatenate([values_in, hop(values_in, 2)], axis=0)
    return jnp.concatenate([beside, hop(beside, 1)], axis=0)


def fold(partial):
    half = partial.shape[0] // 2
    beside = partial[:half] + wide(hop(low(partial[half:]), 1))
    quarter = half // 2
    return beside[:quarter] + wide(hop(low(beside[quarter:]), 2))


def in_order(blocks, rank):
    first, second, third, fourth = blocks
    core = (rank & 1) == 1
    chip = (rank & 2) == 2
    low_pair = (jnp.where(core, third, first), jnp.where(core, first, third))
    high_pair = (jnp.where(core, fourth, second), jnp.where(core, second, fourth))
    return (
        jnp.where(chip, high_pair[0], low_pair[0]),
        jnp.where(chip, high_pair[1], low_pair[1]),
        jnp.where(chip, low_pair[0], high_pair[0]),
        jnp.where(chip, low_pair[1], high_pair[1]),
    )


def ring_of(count):
    return [0] + list(range(1, count, 2)) + [i for i in range(count - 1, 0, -1) if i % 2 == 0]


def ring_next(data_count):
    outer = data_count // 2
    ring = ring_of(outer)
    follow = {ring[i]: ring[(i + 1) % outer] for i in range(outer)}
    return [(z * 2 + y, follow[z] * 2 + y) for z in range(outer) for y in range(2)]


def ring_places(data_count, index):
    outer = data_count // 2
    ring = ring_of(outer)
    table = [[ring[(ring.index(z) - back) % outer] for z in range(outer)] for back in range(outer)]
    return [jnp.asarray(row, jnp.int32)[index // 2] for row in table]


def pair(values_in):
    return lax.ppermute(values_in, "dp", [(i, i ^ 1) for i in range(lax.axis_size("dp"))])


def dp_gather(chunk):
    data_count = lax.axis_size("dp")
    if data_count != 8:
        return lax.all_gather(chunk, "dp", axis=0)
    index = lax.axis_index("dp")
    places = ring_places(data_count, index)
    out = jnp.zeros((data_count,) + chunk.shape, chunk.dtype)
    held = chunk
    follow = ring_next(data_count)
    for step, place in enumerate(places):
        beside = pair(held)
        own_row = place * 2 + index % 2
        other_row = place * 2 + 1 - index % 2
        out = lax.dynamic_update_index_in_dim(out, held, own_row, 0)
        out = lax.dynamic_update_index_in_dim(out, beside, other_row, 0)
        if step + 1 < len(places):
            held = lax.ppermute(held, "dp", follow)
    return out


def dp_sum(blocks):
    data_count = lax.axis_size("dp")
    if data_count != 8:
        return wide(lax.psum_scatter(blocks, "dp", scatter_dimension=0, tiled=False))
    index = lax.axis_index("dp")
    places = ring_places(data_count, index)
    follow = ring_next(data_count)
    carried = None
    for place in places[1:] + places[:1]:
        own = lax.dynamic_index_in_dim(blocks, place * 2 + index % 2, 0, keepdims=False)
        other = lax.dynamic_index_in_dim(blocks, place * 2 + 1 - index % 2, 0, keepdims=False)
        total = wide(own) + wide(pair(other))
        if carried is not None:
            total = total + wide(carried)
        if place is not places[0]:
            carried = lax.ppermute(low(total), "dp", follow)
    return total


def dp_sum_direct(blocks):
    data_count = lax.axis_size("dp")
    if data_count != 8:
        return wide(lax.psum_scatter(blocks, "dp", scatter_dimension=0, tiled=False))
    return jnp.sum(wide(lax.all_to_all(blocks, "dp", 0, 0, tiled=True)), axis=0)


def body(tokens, ln1_gain, w_qkv, w_out, w_ada, w_up, w_down, out_grad, layout, timestep):
    seq_count = lax.axis_size("seq")
    data_count = lax.axis_size("dp")
    rank = lax.axis_index("seq")
    tok_rows, width = tokens.shape
    group_rows = tok_rows * seq_count
    heads_local = HEADS // seq_count
    local_width = heads_local * HEAD_DIM
    rows = w_qkv.shape[0]
    hidden = w_up.shape[1] // seq_count
    down_rows = w_down.shape[0]
    out_piece = w_out.shape[0] // seq_count
    down_piece = down_rows // seq_count

    part_qkv = lax.dynamic_slice(
        w_qkv.reshape(rows, 3, seq_count, local_width),
        (0, 0, rank, 0),
        (rows, 3, 1, local_width),
    ).reshape(rows, 3 * local_width)
    qkv_weight = dp_gather(part_qkv).reshape(width, 3 * local_width)

    joint_there = []
    joint_back = []
    for source in range(data_count * seq_count):
        target = (source % data_count) * seq_count + source // data_count
        joint_there.append((source, target))
        joint_back.append((target, source))
    pieces = jnp.concatenate(
        [
            lax.dynamic_slice_in_dim(w_out, rank * out_piece, out_piece, 0),
            lax.dynamic_slice_in_dim(w_down, rank * down_piece, down_piece, 0),
        ],
        axis=0,
    )
    pieces = lax.ppermute(pieces, ("dp", "seq"), joint_there)
    part_up = lax.dynamic_slice_in_dim(w_up, rank * hidden, hidden, 1)
    gathered = dp_gather(pieces)
    own_out = gathered[:, :out_piece].reshape(-1, width)
    down_weight = gathered[:, out_piece:].reshape(hidden, width)
    up_weight = dp_gather(part_up).reshape(width, hidden)
    out_blocks = spread(own_out)

    embed = low(time_table(wide(timestep), width))
    sent = jnp.stack(
        [embed.reshape(data_count, rows), jnp.broadcast_to(ln1_gain, (data_count, rows))], axis=1
    )
    taken = lax.all_to_all(sent, "dp", 0, 0, tiled=True)
    embeds = taken[:, 0]
    gain = wide(taken[:, 1].reshape(width))
    mod_parts = jnp.dot(embeds, w_ada, preferred_element_type=jnp.float32)
    modulation = jnp.sum(lax.all_to_all(mod_parts, "dp", 0, 0, tiled=True), axis=0)
    mod_scale = modulation[:width]
    mod_shift = modulation[width : 2 * width]
    mod_gate = modulation[2 * width :]

    inputs_all = wide(spread(tokens))
    normed_one, _ = layer_norm(inputs_all)
    hidden_one = low(normed_one * gain)
    masks = jnp.asarray(MASKS, jnp.int32)
    positions = (
        (rank ^ masks)[:, None] * tok_rows + jnp.arange(tok_rows, dtype=jnp.int32)[None, :]
    ).reshape(group_rows)
    cos_table, sine_table = rope_tables(positions)
    projected = jnp.dot(hidden_one, qkv_weight, preferred_element_type=jnp.float32).reshape(
        group_rows, 3, heads_local, HEAD_DIM
    )
    queries = low(rotate(projected[:, 0], cos_table, sine_table, 1.0))
    keys = low(rotate(projected[:, 1], cos_table, sine_table, 1.0))
    values = low(projected[:, 2])
    scores = jnp.einsum("qhd,khd->hqk", queries, keys, preferred_element_type=jnp.float32) * 0.125
    allowed = visible(positions, positions, layout[0, 0], layout[0, 1])
    scores = jnp.where(allowed[None], scores, neg_fill)
    row_max = jnp.max(scores, axis=-1, keepdims=True)
    exponent = jnp.exp(scores - row_max)
    row_sum = jnp.sum(exponent, axis=-1, keepdims=True)
    probs = low(exponent / row_sum)
    attended = low(
        jnp.einsum("hqk,khd->qhd", probs, values, preferred_element_type=jnp.float32)
    ).reshape(group_rows, local_width)
    attended_own = [attended[:tok_rows]] + [
        hop(attended[j * tok_rows : (j + 1) * tok_rows], MASKS[j]) for j in (1, 2, 3)
    ]
    attended_own = jnp.concatenate(attended_own, axis=1)

    inputs = wide(tokens)
    middle = inputs + jnp.dot(attended_own, out_blocks, preferred_element_type=jnp.float32)
    normed_two, scaling_two = layer_norm(middle)
    hidden_two = low(normed_two * (1.0 + mod_scale) + mod_shift)

    hidden_all = spread(hidden_two)
    grad_all = wide(spread(out_grad))
    pre_act = jnp.dot(hidden_all, up_weight, preferred_element_type=jnp.float32)
    gelu_vals, gelu_pull = jax.vjp(lambda inner: jax.nn.gelu(inner, approximate=True), pre_act)
    activated = low(gelu_vals)
    grad_mlp = low(mod_gate * grad_all)
    grad_act = right_product(grad_mlp, down_weight)
    grad_pre = low(gelu_pull(grad_act)[0])
    grad_hidden_two = fold(right_product(grad_pre, up_weight))
    mlp_part = jnp.dot(activated, down_weight, preferred_element_type=jnp.float32)
    grad_gate = jnp.sum(grad_all * mlp_part, axis=0)
    mlp_out = fold(mlp_part)
    result = middle + mod_gate * mlp_out
    grad_wdown = left_product(activated, grad_mlp)
    grad_wup = left_product(hidden_all, grad_pre)

    grad_out = wide(out_grad)
    grad_scale = jnp.sum(grad_hidden_two * normed_two, axis=0)
    grad_shift = jnp.sum(grad_hidden_two, axis=0)
    grad_middle = grad_out + norm_back(grad_hidden_two * (1.0 + mod_scale), normed_two, scaling_two)
    grad_branch = low(grad_middle)
    grad_att = low(right_product(grad_branch, out_blocks))
    grad_att_parts = [grad_att[:, :local_width]] + [
        hop(grad_att[:, j * local_width : (j + 1) * local_width], MASKS[j]) for j in (1, 2, 3)
    ]
    grad_attended = jnp.concatenate(grad_att_parts, axis=0).reshape(
        group_rows, heads_local, HEAD_DIM
    )
    grad_wout = fold(left_product(attended_own, grad_branch))

    grad_mod = jnp.concatenate([grad_scale, grad_shift, grad_gate]).reshape(3, width)
    grad_mod = grad_mod + hop(grad_mod, 1)
    grad_mod = grad_mod + hop(grad_mod, 2)
    grad_mods = lax.all_to_all(
        jnp.broadcast_to(grad_mod[None], (data_count, 3, width)), "dp", 0, 0, tiled=True
    ).reshape(data_count, 3 * width)
    final_ada = lax.dot_general(
        wide(embeds), grad_mods, (((0,), (0,)), ((), ())), precision=lax.Precision.HIGHEST
    )

    value_grad = jnp.einsum("hqk,qhd->khd", probs, grad_attended, preferred_element_type=jnp.float32)
    prob_grad = jnp.einsum("qhd,khd->hqk", grad_attended, values, preferred_element_type=jnp.float32)
    pexp = exponent / row_sum
    row_centre = jnp.sum(pexp * prob_grad, axis=-1, keepdims=True)
    score_grad = low(pexp * (prob_grad - row_centre))
    query_grad = (
        jnp.einsum("hqk,khd->qhd", score_grad, keys, preferred_element_type=jnp.float32) * 0.125
    )
    key_grad = (
        jnp.einsum("hqk,qhd->khd", score_grad, queries, preferred_element_type=jnp.float32) * 0.125
    )
    grad_qkv = jnp.stack(
        [
            rotate(wide(low(query_grad)), cos_table, sine_table, -1.0),
            rotate(wide(low(key_grad)), cos_table, sine_table, -1.0),
            value_grad,
        ],
        axis=1,
    )
    grad_qkv = low(grad_qkv).reshape(group_rows, 3 * local_width)
    grad_wqkv = left_product(hidden_one, grad_qkv)
    grad_hidden_part = right_product(grad_qkv, qkv_weight)
    grad_gain = jnp.sum(grad_hidden_part * normed_one, axis=0)
    grad_hidden_one = fold(grad_hidden_part)
    normed_own, scaling_own = layer_norm(inputs)
    grad_inputs = grad_middle + norm_back(grad_hidden_one * gain, normed_own, scaling_own)

    sum_up = dp_sum(low(grad_wup).reshape(data_count, rows, hidden))
    sum_down = dp_sum(low(grad_wdown).reshape(data_count, down_piece, width))
    sum_out = dp_sum_direct(low(grad_wout).reshape(data_count, out_piece, width))
    gain_rows = jnp.pad(
        low(grad_gain).reshape(data_count, 1, rows), ((0, 0), (0, 0), (0, 3 * local_width - rows))
    )
    sum_qkv = dp_sum_direct(
        jnp.concatenate(
            [low(grad_wqkv).reshape(data_count, rows, 3 * local_width), gain_rows], axis=1
        )
    )
    back = lax.ppermute(
        jnp.concatenate([low(sum_out), low(sum_down)], axis=0), ("dp", "seq"), joint_back
    )

    def to_all(part):
        return [
            wide(block) for block in spread(part).reshape((seq_count,) + part.shape)
        ]

    final_up = jnp.concatenate(in_order(to_all(low(sum_up)), rank), axis=1)
    pieces_back = in_order(to_all(back), rank)
    final_out = jnp.concatenate([block[:out_piece] for block in pieces_back], axis=0)
    final_down = jnp.concatenate([block[out_piece:] for block in pieces_back], axis=0)
    qkv_parts = to_all(low(sum_qkv))
    final_gain = sum(block[rows, :rows] for block in qkv_parts)
    final_qkv = jnp.stack(
        in_order([block[:rows].reshape(rows, 3, local_width) for block in qkv_parts], rank), axis=2
    ).reshape(rows, 3 * width)
    return (
        low(result),
        low(grad_inputs),
        final_gain,
        final_qkv,
        final_out,
        final_ada,
        final_up,
        final_down,
    )


def solution(mesh):
    placed = (
        P(("dp", "seq"), None),
        P("dp"),
        P("dp", None),
        P("dp", None),
        P("dp", None),
        P("dp", None),
        P("dp", None),
        P(("dp", "seq"), None),
        P("dp", None),
        P("dp"),
    )
    return jax.shard_map(
        body,
        mesh=mesh,
        in_specs=placed,
        out_specs=(
            P(("dp", "seq"), None),
            P(("dp", "seq"), None),
            P("dp"),
            P("dp", None),
            P("dp", None),
            P("dp", None),
            P("dp", None),
            P("dp", None),
        ),
        check_vma=False,
    )
```

time: 873 us -> 366 us (0.42)
  waiting for transfers between devices: 565 us -> 101 us
  starting transfers between devices: 15.2 us -> 103 us
  blocking collectives: 86 us -> 0 us
  matrix products: 79.6 us -> 55.5 us
  other arithmetic: 53.6 us -> 40.4 us
  between operations: 17.5 us -> 5.17 us
    all_gather x5 -> x0, waiting for transfers between devices: 238 us -> none  [the longest x1 78.6 us: body(): lax.all_gather(w_up, 'dp', axis=0, tiled=True)]
    reduce_scatter x5 -> x0, waiting for transfers between devices: 216 us -> none  [the longest x1 72.5 us: body(): lax.psum_scatter(parts[1], 'dp', scatter_dimension=0, tiled=True)]
    ppermute x0 -> x67, waiting for transfers between devices: none -> 91.4 us  [the longest x30 44.1 us: hop(): lax.ppermute(values_in, 'seq', [(i, i ^ mask) for i in range(lax.axis_siz...]
    ppermute x0 -> x67, starting transfers between devices: none -> 80.1 us  [the longest x20 22.4 us: pair(): lax.ppermute(values_in, 'dp', [(i, i ^ 1) for i in range(lax.axis_size('d...]
    unnamed x16 -> x0, waiting for transfers between devices: 60.7 us -> none
    unnamed x4 -> x0, blocking collectives: 56.2 us -> none
    all_to_all x4 -> x5, waiting for transfers between devices: 49.5 us -> 9.82 us  [the longest x2 9.82 us: dp_sum_direct(): return jnp.sum(wide(lax.all_to_all(blocks, 'dp', 0, 0, tiled=True)), axis=0)]
    all_gather x4 -> x0, blocking collectives: 29.8 us -> none  [the longest x1 9.05 us: body(): lax.all_gather(owned[1].astype(jnp.bfloat16), 'seq', axis=1, tiled=True)]
  transfers between devices with their start and end apart: 17 -> 72, of which waited for: 13 -> 26; matrix products, arithmetic and copies ran while one was open for 18% -> 37% of each run, Pallas kernels for 0% -> 0%
where the time goes in v1:
time: 366 us; the launch traced here: 360 us
  starting transfers between devices  103 us (28%)
  waiting for transfers between devices  101 us (28%)
  matrix products  55.5 us (15%)
  local copies, waits for them, and re-layouts  54.2 us (15%)
  other arithmetic  40.4 us (11%)
  between operations  5.17 us (1%)
    ppermute x30, waiting for transfers between devices, hop(): lax.ppermute(values_in, 'seq', [(i, i ^ mask) for i in range(lax.axis_siz...  44.1 us
    ppermute x20, starting transfers between devices, pair(): lax.ppermute(values_in, 'dp', [(i, i ^ 1) for i in range(lax.axis_size('d...  22.4 us
    ppermute x30, starting transfers between devices, hop(): lax.ppermute(values_in, 'seq', [(i, i ^ mask) for i in range(lax.axis_siz...  21 us
    ppermute x6, waiting for transfers between devices, dp_sum(): carried = lax.ppermute(low(total), 'dp', follow)  19.9 us
    ppermute x20, waiting for transfers between devices, pair(): lax.ppermute(values_in, 'dp', [(i, i ^ 1) for i in range(lax.axis_size('d...  18.9 us
    ppermute x9, starting transfers between devices, dp_gather(): held = lax.ppermute(held, 'dp', follow)  18.6 us
    ppermute x6, starting transfers between devices, dp_sum(): carried = lax.ppermute(low(total), 'dp', follow)  15.8 us
    unnamed x151, local copies, waits for them, and re-layouts  13.6 us
  transfers between devices with their start and end apart: 72, of which 26 were waited for; matrix products, arithmetic and copies ran while one was open for 37% of the time, Pallas kernels for 0%

profile of v1, /device:TPU:0, one launch (start us, length us, event | category | flops | bytes accessed | tf_op | source)
XLA Modules:
  0.0 359.9 jit_solution(1032369890319887665)
XLA Ops:
  2.9 3.0 collective-permute-start.2
  15.5 3.3 all-to-all-start
  35.6 5.9 %all-to-all-start.1 = ((f32[8,1,2304]{2,1,0:T(1,128)}), f32[8,1,2304]{2,1,0:T(1,128)S(1)}, u32[]{:S(2)}, u32[]{:S(2)}) async-start(f32[8,1,2304]{2,1,0:T(1,128)} %copy.154), calls=%async_computation.1 | async-start | bytes 147456 | tf_op jit(solution)/shard_map/all_to_all | solution.py:240
  44.9 5.7 %collective-permute-start.4 = (bf16[96,576]{0,1:T(8,128)(2,1)}, bf16[96,576]{0,1:T(8,128)(2,1)}, u32[]{:S(2)}, u32[]{:S(2)}) collective-permute-start(bf16[96,576]{0,1:T(8,128)(2,1)} %collective-permute-done.3), channel_id=1, source_target_pairs={{0,4},{4,0},{8,12},{12,8},{16,20},{20,16},{24,28},{28,24},{1,5},{5... | collective-permute-start | bytes 331784 | tf_op jit(solution)/shard_map/ppermute | solution.py:141
  60.6 6.8 %collective-permute-start.7 = (bf16[96,576]{0,1:T(8,128)(2,1)S(1)}, bf16[96,576]{0,1:T(8,128)(2,1)}, u32[]{:S(2)}, u32[]{:S(2)}) collective-permute-start(bf16[96,576]{0,1:T(8,128)(2,1)S(1)} %collective-permute-done.5), channel_id=1, source_target_pairs={{0,8},{4,12},{8,24},{12,28},{16,0},{20,4},{24,16},{28,20},{1,9},{5... | collective-permute-start | bytes 331784 | tf_op jit(solution)/shard_map/ppermute | solution.py:160
  68.0 3.6 collective-permute-start.14
  87.3 5.8 %collective-permute-done.18 = bf16[120,768]{1,0:T(8,128)(2,1)S(1)} collective-permute-done((bf16[120,768]{1,0:T(8,128)(2,1)S(1)}, bf16[120,768]{1,0:T(8,128)(2,1)S(1)}, u32[]{:S(2)}, u32[]{:S(2)}) %collective-permute-start.18) | collective-permute-done | bytes 184352 | tf_op jit(solution)/shard_map/ppermute | solution.py:160
  94.2 4.4 %collective-permute-done.19 = bf16[120,768]{1,0:T(8,128)(2,1)S(1)} collective-permute-done((bf16[120,768]{1,0:T(8,128)(2,1)S(1)}, bf16[120,768]{1,0:T(8,128)(2,1)S(1)}, u32[]{:S(2)}, u32[]{:S(2)}) %collective-permute-start.19) | collective-permute-done | bytes 184352 | tf_op jit(solution)/shard_map/ppermute | solution.py:141
  98.7 6.9 %collective-permute-start.20 = (bf16[192,768]{1,0:T(8,128)(2,1)S(1)}, bf16[192,768]{1,0:T(8,128)(2,1)}, u32[]{:S(2)}, u32[]{:S(2)}) collective-permute-start(bf16[192,768]{1,0:T(8,128)(2,1)S(1)} %bitcast.192), channel_id=1, source_target_pairs={{0,2},{1,3},{2,0},{3,1},{4,6},{5,7},{6,4},{7,5},{8,10},{9,11},{10,... | collective-permute-start | bytes 884744 | tf_op jit(solution)/shard_map/ppermute | solution.py:93
  112.4 8.8 %fusion.125 = (f32[3,1024]{1,0:T(4,128)S(1)}, f32[3,1024,1024]{1,2,0:T(8,128)}) fusion(pred[1024,1024]{0,1:T(8,128)(4,1)} %compare_or_fusion, bf16[1024,3,32]{0,2,1:T(8,128)(2,1)S(1)} %get-tuple-element.58, bf16[1024,3,32]{0,2,1:T(8,128)(2,1)S(1)} %get-tuple-element.59, bf16[1024,3,32]{0,2,1:T(8,128)(2,1)S(1)} %get-tuple-element.35, ...), kind=kOutput, calls=%fused_computation.281 | convolution fusion | flops 416809984 | bytes 14430208 | tf_op jit(solution)/shard_map/sub | solution.py:263
  122.4 6.1 %fusion.47 = bf16[1024,3,64]{0,2,1:T(8,128)(2,1)S(1)} fusion(f32[1024,3,3,64]{0,3,2,1:T(8,128)} %copy-done.27, f32[3,1024,1024]{1,2,0:T(8,128)} %get-tuple-element.73, f32[3,1024]{1,0:T(4,128)S(1)} %get-tuple-element.72), kind=kOutput, calls=%fused_computation.69 | convolution fusion | flops 409141248 | bytes 13381632 | tf_op jit(solution)/shard_map/hqk,khd->qhd/dot_general | solution.py:267
  141.0 12.2 %collective-permute-done.22 = bf16[256,768]{1,0:T(8,128)(2,1)S(1)} collective-permute-done((bf16[256,768]{1,0:T(8,128)(2,1)S(1)}, bf16[256,768]{1,0:T(8,128)(2,1)S(1)}, u32[]{:S(2)}, u32[]{:S(2)}) %collective-permute-start.22) | collective-permute-done | bytes 393248 | tf_op jit(solution)/shard_map/ppermute | solution.py:93
  154.5 5.3 %collective-permute-done.30 = bf16[96,768]{1,0:T(8,128)(2,1)S(1)} collective-permute-done((bf16[96,768]{1,0:T(8,128)(2,1)S(1)}, bf16[96,768]{1,0:T(8,128)(2,1)S(1)}, u32[]{:S(2)}, u32[]{:S(2)}) %collective-permute-start.30) | collective-permute-done | bytes 147488 | tf_op jit(solution)/shard_map/ppermute | solution.py:141
  163.6 4.2 %fusion.20 = bf16[1024,768]{1,0:T(8,128)(2,1)S(1)} fusion(f32[1024,768]{1,0:T(8,128)S(1)} %fusion.65, bf16[768,768]{1,0:T(8,128)(2,1)S(1)} %bitcast.179, f32[768]{0:T(1024)S(1)} %copy-done.57, bf16[512,768]{1,0:T(8,128)(2,1)S(1)} %collective-permute-done.34, bf16[256,768]{1,0:T(8,128)(2,1)S(1)} %collective-permute-done.33, bf16[256,768]{1,0:T(8,128)(2,1)S(1)} %copy-done.13), kind=kOutput, calls=%fused_computation.33 | convolution fusion | flops 1229979648 | bytes 7474176 | tf_op jit(solution)/shard_map/dot_general | solution.py:79
  178.0 3.1 collective-permute-done.49
  182.5 4.2 %collective-permute-done.60 = bf16[96,768]{1,0:T(8,128)(2,1)S(1)} collective-permute-done((bf16[96,768]{1,0:T(8,128)(2,1)S(1)}, bf16[96,768]{1,0:T(8,128)(2,1)S(1)}, u32[]{:S(2)}, u32[]{:S(2)}) %collective-permute-start.60) | collective-permute-done | bytes 147488 | tf_op jit(solution)/shard_map/ppermute | solution.py:141
  187.4 12.2 %collective-permute-start.50 = (bf16[96,768]{1,0:T(8,128)(2,1)S(1)}, bf16[96,768]{1,0:T(8,128)(2,1)S(1)}, u32[]{:S(2)}, u32[]{:S(2)}) collective-permute-start(bf16[96,768]{1,0:T(8,128)(2,1)S(1)} %fusion.79), channel_id=1, source_target_pairs={{0,8},{4,12},{8,24},{12,28},{16,0},{20,4},{24,16},{28,20},{1,9},{5... | collective-permute-start | bytes 442376 | tf_op jit(solution)/shard_map/ppermute | solution.py:179
  200.5 3.8 %collective-permute-done.50 = bf16[96,768]{1,0:T(8,128)(2,1)S(1)} collective-permute-done((bf16[96,768]{1,0:T(8,128)(2,1)S(1)}, bf16[96,768]{1,0:T(8,128)(2,1)S(1)}, u32[]{:S(2)}, u32[]{:S(2)}) %collective-permute-start.50) | collective-permute-done | bytes 147488 | tf_op jit(solution)/shard_map/ppermute | solution.py:179
  205.7 4.6 %collective-permute-done.63 = bf16[96,768]{1,0:T(8,128)(2,1)S(1)} collective-permute-done((bf16[96,768]{1,0:T(8,128)(2,1)S(1)}, bf16[96,768]{1,0:T(8,128)(2,1)S(1)}, u32[]{:S(2)}, u32[]{:S(2)}) %collective-permute-start.63) | collective-permute-done | bytes 147488 | tf_op jit(solution)/shard_map/ppermute | solution.py:179
  211.7 5.9 %collective-permute-done.51 = bf16[96,768]{1,0:T(8,128)(2,1)S(1)} collective-permute-done((bf16[96,768]{1,0:T(8,128)(2,1)S(1)}, bf16[96,768]{1,0:T(8,128)(2,1)S(1)}, u32[]{:S(2)}, u32[]{:S(2)}) %collective-permute-start.51) | collective-permute-done | bytes 147488 | tf_op jit(solution)/shard_map/ppermute | solution.py:179
  219.5 4.2 %collective-permute-done.64 = bf16[96,768]{1,0:T(8,128)(2,1)S(1)} collective-permute-done((bf16[96,768]{1,0:T(8,128)(2,1)S(1)}, bf16[96,768]{1,0:T(8,128)(2,1)S(1)}, u32[]{:S(2)}, u32[]{:S(2)}) %collective-permute-start.64) | collective-permute-done | bytes 147488 | tf_op jit(solution)/shard_map/ppermute | solution.py:179
  234.7 10.2 %collective-permute-done.32 = bf16[256,768]{1,0:T(8,128)(2,1)} collective-permute-done((bf16[256,768]{1,0:T(8,128)(2,1)}, bf16[256,768]{1,0:T(8,128)(2,1)}, u32[]{:S(2)}, u32[]{:S(2)}) %collective-permute-start.32) | collective-permute-done | bytes 393248 | tf_op jit(solution)/shard_map/ppermute | solution.py:93
  258.2 4.0 %all-to-all-start.4 = ((f32[8,3,768]{2,1,0:T(4,128)}), f32[8,3,768]{2,1,0:T(4,128)}, u32[]{:S(2)}, u32[]{:S(2)}) async-start(f32[8,3,768]{2,1,0:T(4,128)} %broadcast_in_dim.168), calls=%async_computation.4 | async-start | bytes 196608 | tf_op jit(solution)/shard_map/all_to_all | solution.py:312
  263.2 6.9 %multiply_reduce_fusion = (f32[3,1024]{1,0:T(4,128)S(1)}, f32[3,1024,1024]{1,2,0:T(8,128)S(1)}) fusion(f32[3,1024,1024]{1,2,0:T(8,128)} %get-tuple-element.73, f32[3,1024]{1,0:T(4,128)S(1)} %copy-done.53, bf16[1024,3,64]{0,2,1:T(8,128)(2,1)} %bitcast.202, f32[1024,3,3,64]{0,3,2,1:T(8,128)} %copy-done.27), kind=kOutput, calls=%fused_computation.2 | convolution fusion | flops 412087296 | bytes 25976832 | tf_op jit(solution)/shard_map/qhd,khd->hqk/dot_general | solution.py:320
  271.8 3.4 multiply_convert_fusion
  275.2 3.0 fusion.43
  285.6 3.0 fusion.10
  295.4 5.6 %all-to-all-start.3 = ((bf16[8,24,768]{2,1,0:T(8,128)(2,1)}), bf16[8,24,768]{2,1,0:T(8,128)(2,1)S(1)}, u32[]{:S(2)}, u32[]{:S(2)}) async-start(bf16[8,24,768]{2,1,0:T(8,128)(2,1)} %bitcast.62), calls=%async_computation.3 | async-start | bytes 589824 | tf_op jit(solution)/shard_map/all_to_all | solution.py:187
  305.5 4.6 %all-to-all-done.3 = bf16[8,24,768]{2,1,0:T(8,128)(2,1)S(1)} async-done(((bf16[8,24,768]{2,1,0:T(8,128)(2,1)}), bf16[8,24,768]{2,1,0:T(8,128)(2,1)S(1)}, u32[]{:S(2)}, u32[]{:S(2)}) %all-to-all-start.3) | async-done | bytes 294944 | tf_op jit(solution)/shard_map/all_to_all | solution.py:187
  310.1 4.5 %all-to-all-start.2 = ((bf16[8,97,576]{2,1,0:T(8,128)(2,1)}), bf16[8,97,576]{2,1,0:T(8,128)(2,1)}, u32[]{:S(2)}, u32[]{:S(2)}) async-start(bf16[8,97,576]{2,1,0:T(8,128)(2,1)} %fusion.50), calls=%async_computation.2 | async-start | bytes 2129920 | tf_op jit(solution)/shard_map/all_to_all | solution.py:187
  325.6 5.7 %collective-permute-done.41 = bf16[256,768]{1,0:T(8,128)(2,1)S(1)} collective-permute-done((bf16[256,768]{1,0:T(8,128)(2,1)S(1)}, bf16[256,768]{1,0:T(8,128)(2,1)S(1)}, u32[]{:S(2)}, u32[]{:S(2)}) %collective-permute-start.41) | collective-permute-done | bytes 393248 | tf_op jit(solution)/shard_map/ppermute | solution.py:93
  334.9 5.2 %all-to-all-done.2 = bf16[8,97,576]{2,1,0:T(8,128)(2,1)} async-done(((bf16[8,97,576]{2,1,0:T(8,128)(2,1)}), bf16[8,97,576]{2,1,0:T(8,128)(2,1)}, u32[]{:S(2)}, u32[]{:S(2)}) %all-to-all-start.2) | async-done | bytes 893984 | tf_op jit(solution)/shard_map/all_to_all | solution.py:187
  (447 shorter events, 178.6 us)
Async XLA Ops:
  2.9 38.6 %collective-permute-start.2 = (bf16[96,576]{0,1:T(8,128)(2,1)S(1)}, bf16[96,576]{0,1:T(8,128)(2,1)}, u32[]{:S(2)}, u32[]{:S(2)}) collective-permute-start(bf16[96,576]{0,1:T(8,128)(2,1)S(1)} %bitcast.197), channel_id=1, source_target_pairs={{0,4},{4,0},{8,12},{12,8},{16,20},{20,16},{24,28},{28,24},{1,5},{5... | collective-permute-start | bytes 331784 | tf_op jit(solution)/shard_map/ppermute | solution.py:141
  6.0 37.9 %collective-permute-start.3 = (bf16[96,576]{0,1:T(8,128)(2,1)S(1)}, bf16[96,576]{0,1:T(8,128)(2,1)}, u32[]{:S(2)}, u32[]{:S(2)}) collective-permute-start(bf16[96,576]{0,1:T(8,128)(2,1)S(1)} %bitcast.198), channel_id=1, source_target_pairs={{0,8},{4,12},{8,24},{12,28},{16,0},{20,4},{24,16},{28,20},{1,9},{5... | collective-permute-start | bytes 331784 | tf_op jit(solution)/shard_map/ppermute | solution.py:160
  9.2 42.7 %collective-permute-start.24 = (bf16[96,768]{1,0:T(8,128)(2,1)}, bf16[96,768]{1,0:T(8,128)(2,1)}, u32[]{:S(2)}, u32[]{:S(2)}) collective-permute-start(bf16[96,768]{1,0:T(8,128)(2,1)} %get-tuple-element.15), channel_id=1, source_target_pairs={{0,4},{4,0},{8,12},{12,8},{16,20},{20,16},{24,28},{28,24},{1,5},{5... | collective-permute-start | bytes 442376 | tf_op jit(solution)/shard_map/ppermute | solution.py:141
  9.7 42.2 %collective-permute-start.25 = (bf16[96,768]{1,0:T(8,128)(2,1)}, bf16[96,768]{1,0:T(8,128)(2,1)}, u32[]{:S(2)}, u32[]{:S(2)}) collective-permute-start(bf16[96,768]{1,0:T(8,128)(2,1)} %get-tuple-element.15), channel_id=1, source_target_pairs={{0,8},{4,12},{8,24},{12,28},{16,0},{20,4},{24,16},{28,20},{1,9},{5... | collective-permute-start | bytes 442376 | tf_op jit(solution)/shard_map/ppermute | solution.py:160
  12.5 67.7 %collective-permute-start = (bf16[256,768]{0,1:T(8,128)(2,1)S(1)}, bf16[256,768]{0,1:T(8,128)(2,1)S(1)}, u32[]{:S(2)}, u32[]{:S(2)}) collective-permute-start(bf16[256,768]{0,1:T(8,128)(2,1)S(1)} %copy.139), channel_id=1, source_target_pairs={{0,2},{1,3},{2,0},{3,1},{4,6},{5,7},{6,4},{7,5},{8,10},{9,11},{10,... | collective-permute-start | bytes 1179656 | tf_op jit(solution)/shard_map/ppermute | solution.py:93
  15.5 18.0 %all-to-all-start = ((bf16[8,2,96]{2,1,0:T(2,128)(2,1)}), bf16[8,2,96]{2,1,0:T(2,128)(2,1)S(1)}, u32[]{:S(2)}, u32[]{:S(2)}) async-start(bf16[8,2,96]{2,1,0:T(2,128)(2,1)} %copy.140), calls=%async_computation | async-start | bytes 8192 | tf_op jit(solution)/shard_map/all_to_all | solution.py:236
  35.6 15.7 %all-to-all-start.1 = ((f32[8,1,2304]{2,1,0:T(1,128)}), f32[8,1,2304]{2,1,0:T(1,128)S(1)}, u32[]{:S(2)}, u32[]{:S(2)}) async-start(f32[8,1,2304]{2,1,0:T(1,128)} %copy.154), calls=%async_computation.1 | async-start | bytes 147456 | tf_op jit(solution)/shard_map/all_to_all | solution.py:240
  41.5 12.9 %collective-permute-start.12 = (bf16[120,768]{1,0:T(8,128)(2,1)S(1)}, bf16[120,768]{1,0:T(8,128)(2,1)S(1)}, u32[]{:S(2)}, u32[]{:S(2)}) collective-permute-start(bf16[120,768]{1,0:T(8,128)(2,1)S(1)} %pad_maximum_fusion.23), channel_id=1, source_target_pairs={{0,0},{1,4},{2,8},{3,12},{4,16},{5,20},{6,24},{7,28},{8,1},{9,5},{... | collective-permute-start | bytes 552968 | tf_op jit(solution)/shard_map/ppermute | solution.py:224
  51.9 79.8 %collective-permute-start.27 = (bf16[96,768]{1,0:T(8,128)(2,1)}, bf16[96,768]{1,0:T(8,128)(2,1)}, u32[]{:S(2)}, u32[]{:S(2)}) collective-permute-start(bf16[96,768]{1,0:T(8,128)(2,1)} %collective-permute-done.25), channel_id=1, source_target_pairs={{0,8},{4,12},{8,24},{12,28},{16,0},{20,4},{24,16},{28,20},{1,9},{5... | collective-permute-start | bytes 442376 | tf_op jit(solution)/shard_map/ppermute | solution.py:160
  55.4 21.8 %collective-permute-start.13 = (bf16[120,768]{1,0:T(8,128)(2,1)S(1)}, bf16[120,768]{1,0:T(8,128)(2,1)}, u32[]{:S(2)}, u32[]{:S(2)}) collective-permute-start(bf16[120,768]{1,0:T(8,128)(2,1)S(1)} %collective-permute-done.12), channel_id=1, source_target_pairs={{0,4},{4,0},{8,12},{12,8},{16,20},{20,16},{24,28},{28,24},{1,5},{5... | collective-permute-start | bytes 552968 | tf_op jit(solution)/shard_map/ppermute | solution.py:141
  81.2 24.3 %collective-permute-start.1 = (bf16[512,768]{0,1:T(8,128)(2,1)}, bf16[512,768]{0,1:T(8,128)(2,1)}, u32[]{:S(2)}, u32[]{:S(2)}) collective-permute-start(bf16[512,768]{0,1:T(8,128)(2,1)} %pad_maximum_fusion.7), channel_id=1, source_target_pairs={{0,1},{1,0},{2,3},{3,2},{4,5},{5,4},{6,7},{7,6},{8,9},{9,8},{10,11... | collective-permute-start | bytes 2359304 | tf_op jit(solution)/shard_map/ppermute | solution.py:93
  98.7 22.6 %collective-permute-start.20 = (bf16[192,768]{1,0:T(8,128)(2,1)S(1)}, bf16[192,768]{1,0:T(8,128)(2,1)}, u32[]{:S(2)}, u32[]{:S(2)}) collective-permute-start(bf16[192,768]{1,0:T(8,128)(2,1)S(1)} %bitcast.192), channel_id=1, source_target_pairs={{0,2},{1,3},{2,0},{3,1},{4,6},{5,7},{6,4},{7,5},{8,10},{9,11},{10,... | collective-permute-start | bytes 884744 | tf_op jit(solution)/shard_map/ppermute | solution.py:93
  122.3 15.3 %collective-permute-start.21 = (bf16[384,768]{1,0:T(8,128)(2,1)S(1)}, bf16[384,768]{1,0:T(8,128)(2,1)S(1)}, u32[]{:S(2)}, u32[]{:S(2)}) collective-permute-start(bf16[384,768]{1,0:T(8,128)(2,1)S(1)} %pad_maximum_fusion.12), channel_id=1, source_target_pairs={{0,1},{1,0},{2,3},{3,2},{4,5},{5,4},{6,7},{7,6},{8,9},{9,8},{10,11... | collective-permute-start | bytes 1769480 | tf_op jit(solution)/shard_map/ppermute | solution.py:93
  131.8 21.5 %collective-permute-start.33 = (bf16[256,768]{1,0:T(8,128)(2,1)S(1)}, bf16[256,768]{1,0:T(8,128)(2,1)S(1)}, u32[]{:S(2)}, u32[]{:S(2)}) collective-permute-start(bf16[256,768]{1,0:T(8,128)(2,1)S(1)} %copy-done.13), channel_id=1, source_target_pairs={{0,2},{1,3},{2,0},{3,1},{4,6},{5,7},{6,4},{7,5},{8,10},{9,11},{10,... | collective-permute-start | bytes 1179656 | tf_op jit(solution)/shard_map/ppermute | solution.py:93
  134.0 20.5 %collective-permute-start.28 = (bf16[96,768]{1,0:T(8,128)(2,1)}, bf16[96,768]{1,0:T(8,128)(2,1)S(1)}, u32[]{:S(2)}, u32[]{:S(2)}) collective-permute-start(bf16[96,768]{1,0:T(8,128)(2,1)} %collective-permute-done.27), channel_id=1, source_target_pairs={{0,4},{4,0},{8,12},{12,8},{16,20},{20,16},{24,28},{28,24},{1,5},{5... | collective-permute-start | bytes 442376 | tf_op jit(solution)/shard_map/ppermute | solution.py:141
  136.6 17.4 %collective-permute-start.29 = (bf16[96,768]{1,0:T(8,128)(2,1)}, bf16[96,768]{1,0:T(8,128)(2,1)S(1)}, u32[]{:S(2)}, u32[]{:S(2)}) collective-permute-start(bf16[96,768]{1,0:T(8,128)(2,1)} %collective-permute-done.27), channel_id=1, source_target_pairs={{0,8},{4,12},{8,24},{12,28},{16,0},{20,4},{24,16},{28,20},{1,9},{5... | collective-permute-start | bytes 442376 | tf_op jit(solution)/shard_map/ppermute | solution.py:160
  139.8 13.4 %collective-permute-start.22 = (bf16[256,768]{1,0:T(8,128)(2,1)S(1)}, bf16[256,768]{1,0:T(8,128)(2,1)S(1)}, u32[]{:S(2)}, u32[]{:S(2)}) collective-permute-start(bf16[256,768]{1,0:T(8,128)(2,1)S(1)} %add_convert_fusion), channel_id=1, source_target_pairs={{0,2},{1,3},{2,0},{3,1},{4,6},{5,7},{6,4},{7,5},{8,10},{9,11},{10,... | collective-permute-start | bytes 1179656 | tf_op jit(solution)/shard_map/ppermute | solution.py:93
  163.5 66.3 %collective-permute-start.31 = (bf16[512,768]{1,0:T(8,128)(2,1)S(1)}, bf16[512,768]{1,0:T(8,128)(2,1)S(1)}, u32[]{:S(2)}, u32[]{:S(2)}) collective-permute-start(bf16[512,768]{1,0:T(8,128)(2,1)S(1)} %slice.459), channel_id=1, source_target_pairs={{0,1},{1,0},{2,3},{3,2},{4,5},{5,4},{6,7},{7,6},{8,9},{9,8},{10,11... | collective-permute-start | bytes 2359304 | tf_op jit(solution)/shard_map/ppermute | solution.py:93
  169.3 56.7 %collective-permute-start.35 = (bf16[512,768]{1,0:T(8,128)(2,1)S(1)}, bf16[512,768]{1,0:T(8,128)(2,1)S(1)}, u32[]{:S(2)}, u32[]{:S(2)}) collective-permute-start(bf16[512,768]{1,0:T(8,128)(2,1)S(1)} %slice.458), channel_id=1, source_target_pairs={{0,1},{1,0},{2,3},{3,2},{4,5},{5,4},{6,7},{7,6},{8,9},{9,8},{10,11... | collective-permute-start | bytes 2359304 | tf_op jit(solution)/shard_map/ppermute | solution.py:93
  175.6 24.1 %collective-permute-start.48 = (bf16[96,768]{1,0:T(8,128)(2,1)S(1)}, bf16[96,768]{1,0:T(8,128)(2,1)S(1)}, u32[]{:S(2)}, u32[]{:S(2)}) collective-permute-start(bf16[96,768]{1,0:T(8,128)(2,1)S(1)} %get-tuple-element.24), channel_id=1, source_target_pairs={{0,4},{4,0},{8,12},{12,8},{16,20},{20,16},{24,28},{28,24},{1,5},{5... | collective-permute-start | bytes 442376 | tf_op jit(solution)/shard_map/ppermute | solution.py:141
  186.7 23.7 %collective-permute-start.47 = (bf16[96,768]{1,0:T(8,128)(2,1)S(1)}, bf16[96,768]{1,0:T(8,128)(2,1)S(1)}, u32[]{:S(2)}, u32[]{:S(2)}) collective-permute-start(bf16[96,768]{1,0:T(8,128)(2,1)S(1)} %get-tuple-element.25), channel_id=1, source_target_pairs={{0,4},{4,0},{8,12},{12,8},{16,20},{20,16},{24,28},{28,24},{1,5},{5... | collective-permute-start | bytes 442376 | tf_op jit(solution)/shard_map/ppermute | solution.py:141
  187.4 16.8 %collective-permute-start.50 = (bf16[96,768]{1,0:T(8,128)(2,1)S(1)}, bf16[96,768]{1,0:T(8,128)(2,1)S(1)}, u32[]{:S(2)}, u32[]{:S(2)}) collective-permute-start(bf16[96,768]{1,0:T(8,128)(2,1)S(1)} %fusion.79), channel_id=1, source_target_pairs={{0,8},{4,12},{8,24},{12,28},{16,0},{20,4},{24,16},{28,20},{1,9},{5... | collective-permute-start | bytes 442376 | tf_op jit(solution)/shard_map/ppermute | solution.py:179
  204.9 19.0 %collective-permute-start.46 = (bf16[96,768]{1,0:T(8,128)(2,1)S(1)}, bf16[96,768]{1,0:T(8,128)(2,1)S(1)}, u32[]{:S(2)}, u32[]{:S(2)}) collective-permute-start(bf16[96,768]{1,0:T(8,128)(2,1)S(1)} %get-tuple-element.22), channel_id=1, source_target_pairs={{0,4},{4,0},{8,12},{12,8},{16,20},{20,16},{24,28},{28,24},{1,5},{5... | collective-permute-start | bytes 442376 | tf_op jit(solution)/shard_map/ppermute | solution.py:141
  229.8 84.8 %collective-permute-start.66 = (bf16[192,768]{1,0:T(8,128)(2,1)}, bf16[192,768]{1,0:T(8,128)(2,1)}, u32[]{:S(2)}, u32[]{:S(2)}) collective-permute-start(bf16[192,768]{1,0:T(8,128)(2,1)} %pad_maximum_fusion.21), channel_id=1, source_target_pairs={{0,1},{1,0},{2,3},{3,2},{4,5},{5,4},{6,7},{7,6},{8,9},{9,8},{10,11... | collective-permute-start | bytes 884744 | tf_op jit(solution)/shard_map/ppermute | solution.py:93
  234.6 16.9 %collective-permute-start.56 = (f32[3,768]{1,0:T(4,128)S(1)}, f32[3,768]{1,0:T(4,128)S(1)}, u32[]{:S(2)}, u32[]{:S(2)}) collective-permute-start(f32[3,768]{1,0:T(4,128)S(1)} %reshape.604), channel_id=1, source_target_pairs={{0,1},{1,0},{2,3},{3,2},{4,5},{5,4},{6,7},{7,6},{8,9},{9,8},{10,11... | collective-permute-start | bytes 27656 | tf_op jit(solution)/shard_map/ppermute | solution.py:93
  249.2 12.9 %collective-permute-start.37 = (bf16[256,192]{1,0:T(8,128)(2,1)S(1)}, bf16[256,192]{1,0:T(8,128)(2,1)S(1)}, u32[]{:S(2)}, u32[]{:S(2)}) collective-permute-start(bf16[256,192]{1,0:T(8,128)(2,1)S(1)} %get-tuple-element.51), channel_id=1, source_target_pairs={{0,2},{1,3},{2,0},{3,1},{4,6},{5,7},{6,4},{7,5},{8,10},{9,11},{10,... | collective-permute-start | bytes 294920 | tf_op jit(solution)/shard_map/ppermute | solution.py:93
  249.6 12.6 %collective-permute-start.39 = (bf16[256,192]{1,0:T(8,128)(2,1)S(1)}, bf16[256,192]{1,0:T(8,128)(2,1)S(1)}, u32[]{:S(2)}, u32[]{:S(2)}) collective-permute-start(bf16[256,192]{1,0:T(8,128)(2,1)S(1)} %get-tuple-element.49), channel_id=1, source_target_pairs={{0,3},{1,2},{2,1},{3,0},{4,7},{5,6},{6,5},{7,4},{8,11},{9,10},{10,... | collective-permute-start | bytes 294920 | tf_op jit(solution)/shard_map/ppermute | solution.py:93
  257.5 24.6 %collective-permute-start.44 = (bf16[384,768]{1,0:T(8,128)(2,1)}, bf16[384,768]{1,0:T(8,128)(2,1)}, u32[]{:S(2)}, u32[]{:S(2)}) collective-permute-start(bf16[384,768]{1,0:T(8,128)(2,1)} %slice.460), channel_id=1, source_target_pairs={{0,1},{1,0},{2,3},{3,2},{4,5},{5,4},{6,7},{7,6},{8,9},{9,8},{10,11... | collective-permute-start | bytes 1769480 | tf_op jit(solution)/shard_map/ppermute | solution.py:93
  258.2 37.2 %all-to-all-start.4 = ((f32[8,3,768]{2,1,0:T(4,128)}), f32[8,3,768]{2,1,0:T(4,128)}, u32[]{:S(2)}, u32[]{:S(2)}) async-start(f32[8,3,768]{2,1,0:T(4,128)} %broadcast_in_dim.168), calls=%async_computation.4 | async-start | bytes 196608 | tf_op jit(solution)/shard_map/all_to_all | solution.py:312
  291.5 28.2 %collective-permute-start.40 = (bf16[512,768]{1,0:T(8,128)(2,1)}, bf16[512,768]{1,0:T(8,128)(2,1)}, u32[]{:S(2)}, u32[]{:S(2)}) collective-permute-start(bf16[512,768]{1,0:T(8,128)(2,1)} %copy.177), channel_id=1, source_target_pairs={{0,1},{1,0},{2,3},{3,2},{4,5},{5,4},{6,7},{7,6},{8,9},{9,8},{10,11... | collective-permute-start | bytes 2359304 | tf_op jit(solution)/shard_map/ppermute | solution.py:93
  295.4 14.8 %all-to-all-start.3 = ((bf16[8,24,768]{2,1,0:T(8,128)(2,1)}), bf16[8,24,768]{2,1,0:T(8,128)(2,1)S(1)}, u32[]{:S(2)}, u32[]{:S(2)}) async-start(bf16[8,24,768]{2,1,0:T(8,128)(2,1)} %bitcast.62), calls=%async_computation.3 | async-start | bytes 589824 | tf_op jit(solution)/shard_map/all_to_all | solution.py:187
  310.1 29.9 %all-to-all-start.2 = ((bf16[8,97,576]{2,1,0:T(8,128)(2,1)}), bf16[8,97,576]{2,1,0:T(8,128)(2,1)}, u32[]{:S(2)}, u32[]{:S(2)}) async-start(bf16[8,97,576]{2,1,0:T(8,128)(2,1)} %fusion.50), calls=%async_computation.2 | async-start | bytes 2129920 | tf_op jit(solution)/shard_map/all_to_all | solution.py:187
  (112 other events, 987.8 us)

commit v2 on v1

v2 whole, which is shorter than its diff:
```python
import functools
import math

import jax
import jax.numpy as jnp
from jax import lax
from jax.experimental import pallas as pl
from jax.experimental.pallas import tpu as pltpu
from jax.sharding import PartitionSpec as P

HEADS = 12
HEAD_DIM = 64

eps = 1e-05

MASKS = (0, 2, 1, 3)


def time_table(time_steps, model_width):
    half_dim = model_width // 2
    frequency = jnp.exp(-math.log(10000.0) * jnp.arange(half_dim, dtype=jnp.float32) / half_dim)
    angles = time_steps[:, None] * frequency[None, :]
    return jnp.concatenate([jnp.cos(angles), jnp.sin(angles)], axis=1)


def low(values_in):
    return values_in.astype(jnp.bfloat16)


def wide(values_in):
    return values_in.astype(jnp.float32)


HEAD_TILE = 128
COST = 6.0
MASK_FILL = -1e30
GELU_IN = math.sqrt(2.0 / math.pi)
GELU_CUBE = 0.044715


def rope_tables(positions):
    half_dim = HEAD_DIM // 2
    column = jnp.arange(2 * HEAD_DIM, dtype=jnp.int32)
    frequency = jnp.exp(
        -math.log(10000.0) * 2.0 * (column % half_dim).astype(jnp.float32) / HEAD_DIM
    )
    angles = positions.astype(jnp.float32)[:, None] * frequency[None, :]
    sign = jnp.where(column % HEAD_DIM < half_dim, -1.0, 1.0)
    return (jnp.cos(angles), jnp.sin(angles) * sign[None, :])


def dot_nn(left, right):
    return lax.dot_general(
        left, right, (((1,), (0,)), ((), ())), preferred_element_type=jnp.float32
    )


def dot_nt(left, right):
    return lax.dot_general(
        left, right, (((1,), (1,)), ((), ())), preferred_element_type=jnp.float32
    )


def dot_tn(left, right):
    return lax.dot_general(
        left, right, (((0,), (0,)), ((), ())), preferred_element_type=jnp.float32
    )


def norm_rows(values_in):
    average = jnp.mean(values_in, axis=-1, keepdims=True)
    centred = values_in - average
    variance = jnp.mean(centred * centred, axis=-1, keepdims=True)
    scaling = lax.rsqrt(variance + eps)
    return (centred * scaling, scaling)


def swap_halves(values_in):
    column = lax.broadcasted_iota(jnp.int32, values_in.shape, 1)
    ahead = pltpu.roll(values_in, HEAD_TILE - HEAD_DIM // 2, 1)
    behind = pltpu.roll(values_in, HEAD_DIM // 2, 1)
    return jnp.where(column % HEAD_DIM < HEAD_DIM // 2, ahead, behind)


def whole(count):
    return [pl.BlockSpec(memory_space=pltpu.VMEM)] * count


def scalars():
    return [pl.BlockSpec(memory_space=pltpu.SMEM)]


def run(kernel, out_shapes, args, flops, scratch=(), name=None):
    nbytes = sum(a.size * a.dtype.itemsize for a in args)
    nbytes += sum(math.prod(o.shape) * o.dtype.itemsize for o in out_shapes)
    call = pl.pallas_call(
        kernel,
        out_shape=out_shapes,
        in_specs=scalars() + whole(len(args) - 1),
        out_specs=whole(len(out_shapes)),
        scratch_shapes=list(scratch),
        cost_estimate=pl.CostEstimate(flops=int(flops * COST), bytes_accessed=int(nbytes * COST), transcendentals=0),
        name=name,
    )
    return call(*args)


def shaped(shape, kind=jnp.bfloat16):
    return jax.ShapeDtypeStruct(shape, kind)


FIRST, OWNER, BLOCK, PLACE = 2, 6, 10, 14


def block_segment(info, block, rows, axis):
    shape = (rows, 1) if axis == 0 else (1, rows)
    position = info[FIRST + block] + lax.broadcasted_iota(jnp.int32, shape, axis)
    return (position >= info[0]).astype(jnp.int32) + (position >= info[1]).astype(jnp.int32)


def place_rows(info, chunks, first, rows, dest):
    for index, chunk in enumerate(chunks):
        at = pl.multiple_of(info[PLACE + index] * rows, rows)
        dest[pl.ds(at, rows), : chunk.shape[1]] = chunk[first : first + rows, :]


def first_part_kernel(info, qkv_ref, out_ref, dest):
    span = dest.shape[1] // 4
    for part in range(4):

        @pl.when(info[0] == part)
        def _():
            for third in range(3):
                at = (third * 4 + part) * span
                dest[:, third * span : (third + 1) * span] = qkv_ref[:, at : at + span]
            dest[:, 3 * span :] = out_ref[:, part * span : (part + 1) * span]


def second_part_kernel(count, info, up_ref, down_ref, dest):
    rows = up_ref.shape[0]
    piece = down_ref.shape[0] // 4
    for part in range(4):

        @pl.when(info[0] == part)
        def _():
            for index in range(count):
                at = (index * 4 + part) * piece
                dest[:rows, index * piece : (index + 1) * piece] = up_ref[:, at : at + piece]
            dest[rows:, :] = down_ref[part * piece : (part + 1) * piece, :]


def qkv_kernel(heads, count, info, *refs):
    gain, cos_ref, sin_ref = refs[:3]
    tok_refs = refs[3:7]
    chunks = refs[7 : 7 + count]
    hidden_ref, weight_ref, own_ref, q_ref, k_ref, v_ref = refs[7 + count :]
    rows, width = tok_refs[0].shape
    lw = heads * HEAD_DIM
    place_rows(info, chunks, 0, width // count, weight_ref)
    own_ref[...] = weight_ref[:, 3 * lw : 4 * lw]
    gain_row = gain[...]
    for block in range(4):
        normed, _ = norm_rows(wide(tok_refs[block][...]))
        hidden = low(normed * gain_row)
        here = slice(block * rows, (block + 1) * rows)
        hidden_ref[here, :] = hidden
        both = dot_nn(hidden, weight_ref[:, : 2 * lw])
        last = dot_nn(hidden, weight_ref[:, 2 * lw : 2 * lw + 2 * HEAD_TILE])
        cos_part = cos_ref[here, :]
        sin_part = sin_ref[here, :]
        turned = []
        for tile in range(2 * lw // HEAD_TILE):
            piece = both[:, tile * HEAD_TILE : (tile + 1) * HEAD_TILE]
            turned.append(piece * cos_part + swap_halves(piece) * sin_part)
        column = lax.broadcasted_iota(jnp.int32, (rows, HEAD_TILE), 1)
        segment = block_segment(info, block, rows, 0)
        first_fill = jnp.where(segment == 1, 0.0, MASK_FILL)
        second_fill = jnp.where(segment == 2, 0.0, MASK_FILL)
        q_mark = jnp.where(
            column == HEAD_DIM, first_fill, jnp.where(column == HEAD_DIM + 1, second_fill, 0.0)
        )
        first_mark = jnp.where(segment == 1, 1.0, 0.0)
        second_mark = jnp.where(segment == 2, 1.0, 0.0)
        k_mark = jnp.where(
            column == HEAD_DIM,
            first_mark,
            jnp.where(
                column == HEAD_DIM + 1, second_mark, jnp.where(column < HEAD_DIM + 5, 1.0, 0.0)
            ),
        )
        v_mark = jnp.where(column < HEAD_DIM + 2, 1.0, 0.0)
        for head in range(heads):
            q_at, k_at = head, heads + head
            q_tile = turned[q_at // 2]
            k_tile = turned[k_at // 2]
            v_tile = last[:, HEAD_TILE * (head // 2) : HEAD_TILE * (head // 2 + 1)]
            if q_at % 2:
                q_tile = pltpu.roll(q_tile, HEAD_DIM, 1)
            if k_at % 2:
                k_tile = pltpu.roll(k_tile, HEAD_DIM, 1)
            if head % 2:
                v_tile = pltpu.roll(v_tile, HEAD_DIM, 1)
            there = slice(head * HEAD_TILE, (head + 1) * HEAD_TILE)
            q_ref[here, there] = low(jnp.where(column < HEAD_DIM, q_tile * 0.125, q_mark))
            k_ref[here, there] = low(jnp.where(column < HEAD_DIM, k_tile, k_mark))
            v_ref[here, there] = low(jnp.where(column < HEAD_DIM, v_tile, v_mark))


def attend_kernel(heads, rows, info, q_ref, k_ref, v_ref, *outs):
    att_refs = outs[:4]
    stat_ref = outs[4]
    for block in range(4):
        here = slice(block * rows, (block + 1) * rows)
        column = lax.broadcasted_iota(jnp.int32, (rows, HEAD_TILE), 1)
        results = []
        for head in range(heads):
            there = slice(head * HEAD_TILE, (head + 1) * HEAD_TILE)
            queries = q_ref[here, there]
            scores = dot_nt(queries, k_ref[:, there])
            row_max = jnp.max(scores, axis=-1, keepdims=True)
            weights = low(jnp.exp(scores - row_max))
            summed = dot_nn(weights, v_ref[:, there])
            row_sum = summed[:, HEAD_DIM : HEAD_DIM + 1]
            results.append(summed / row_sum)
            minus = -(row_max + jnp.log(row_sum))
            first = low(minus)
            second = low(minus - wide(first))
            third = low(minus - wide(first) - wide(second))
            stat_ref[here, there] = jnp.where(
                column == HEAD_DIM + 2,
                first,
                jnp.where(
                    column == HEAD_DIM + 3, second, jnp.where(column == HEAD_DIM + 4, third, queries)
                ),
            )
        for head in range(0, heads, 2):
            if head + 1 < heads:
                both = jnp.where(
                    column < HEAD_DIM, results[head], pltpu.roll(results[head + 1], HEAD_DIM, 1)
                )
                att_refs[block][:, head * HEAD_DIM : (head + 2) * HEAD_DIM] = low(both)
            else:
                att_refs[block][:, head * HEAD_DIM :] = low(results[head][:, :HEAD_DIM])


def natural(info, blocks, dest):
    for block in range(4):
        dest[info[OWNER + block]] = blocks[block][...]


def middle_kernel(info, tok_ref, mod_ref, *refs):
    middle_ref, hidden_ref, att_ref, weight_ref = refs[8:]
    natural(info, refs[:4], weight_ref)
    natural(info, refs[4:8], att_ref)
    span = weight_ref.shape[2]
    for columns in range(4):
        there = slice(columns * span, (columns + 1) * span)
        total = wide(tok_ref[:, there])
        for part in range(4):
            total = total + dot_nn(
                att_ref[part], weight_ref[columns, part * span : (part + 1) * span, :]
            )
        middle_ref[:, there] = total
    normed, _ = norm_rows(middle_ref[...])
    hidden_ref[...] = low(normed * (1.0 + mod_ref[0:1, :]) + mod_ref[1:2, :])


def act_grad_kernel(count, skip, info, mod_ref, *refs):
    dy_refs = refs[:4]
    chunks = refs[4 : 4 + count]
    mlp_ref, act_ref, weight_ref = refs[4 + count :]
    rows = dy_refs[0].shape[0]
    place_rows(info, chunks, skip, weight_ref.shape[0] // count, weight_ref)
    gate = mod_ref[2:3, :]
    for block in range(4):
        here = slice(block * rows, (block + 1) * rows)
        grad_mlp = low(gate * wide(dy_refs[block][...]))
        mlp_ref[here, :] = grad_mlp
        act_ref[here, :] = low(dot_nt(grad_mlp, weight_ref[...]))


def forward_kernel(count, info, act_grad, *refs):
    hid_refs = refs[:4]
    chunks = refs[4 : 4 + count]
    act_ref, pre_ref, near_ref, far_ref, weight_ref = refs[4 + count :]
    rows = hid_refs[0].shape[0]
    place_rows(info, chunks, 0, weight_ref.shape[0] // count, weight_ref)
    for block in (2, 3, 1, 0):
        here = slice(block * rows, (block + 1) * rows)
        pre = dot_nn(hid_refs[block][...], weight_ref[...])
        square = pre * pre
        inner = jnp.tanh(GELU_IN * (pre + GELU_CUBE * (square * pre)))
        half = 0.5 * (1.0 + inner)
        act_ref[here, :] = low(pre * half)
        slope = half + 0.5 * pre * (1.0 - inner * inner) * (
            GELU_IN * (1.0 + 3.0 * GELU_CUBE * square)
        )
        grad_pre = low(wide(act_grad[here, :]) * slope)
        pre_ref[here, :] = grad_pre
        dest = near_ref if block < 2 else far_ref
        dest[(block % 2) * rows : (block % 2 + 1) * rows, :] = low(
            dot_nt(grad_pre, weight_ref[...])
        )


def weight_grad_kernel(count, info, act_ref, mlp_ref, pre_ref, *refs):
    hid_refs = refs[:4]
    outs = refs[4:-1]
    sums_ref = refs[-1]
    rows = hid_refs[0].shape[0]
    per = act_ref.shape[1] // count
    up = dot_tn(hid_refs[0][...], pre_ref[:rows, :])
    for block in range(1, 4):
        up = up + dot_tn(hid_refs[block][...], pre_ref[block * rows : (block + 1) * rows, :])
    for index in range(count):
        sums_ref[index, :per, :] = low(up[index * per : (index + 1) * per, :])
    down = dot_tn(act_ref[...], mlp_ref[...])
    for index in range(count):
        sums_ref[index, per:, :] = low(down[index * per : (index + 1) * per, :])
    if len(outs) == 1:
        outs[0][...] = sums_ref[...]
    else:
        for index in range(count):
            outs[index][...] = sums_ref[info[PLACE + index]]


def down_kernel(count, skip, info, act_ref, *refs):
    dy_refs = refs[:4]
    chunks = refs[4 : 4 + count]
    near_ref, far_ref, gate_ref, weight_ref = refs[4 + count :]
    rows = dy_refs[0].shape[0]
    place_rows(info, chunks, skip, weight_ref.shape[0] // count, weight_ref)
    total = jnp.zeros(gate_ref.shape, jnp.float32)
    for block in (2, 3, 1, 0):
        here = slice(block * rows, (block + 1) * rows)
        part = dot_nn(act_ref[here, :], weight_ref[...])
        total = total + jnp.sum(wide(dy_refs[block][...]) * part, axis=0, keepdims=True)
        dest = near_ref if block < 2 else far_ref
        dest[(block % 2) * rows : (block % 2 + 1) * rows, :] = low(part)
    gate_ref[...] = total


def branch_kernel(info, mod_ref, middle_ref, dy_ref, own_ref, core_ref, chip_ref, *refs):
    mid_ref, branch_ref, sums_ref = refs[4:7]
    att_refs = refs[7:11]
    weight_ref = refs[11]
    natural(info, refs[:4], weight_ref)
    rows = dy_ref.shape[0]
    grad_hidden = wide(own_ref[:rows, :]) + wide(core_ref[:rows, :]) + wide(chip_ref[...])
    normed, scaling = norm_rows(middle_ref[...])
    sums_ref[0:1, :] = jnp.sum(grad_hidden * normed, axis=0, keepdims=True)
    sums_ref[1:2, :] = jnp.sum(grad_hidden, axis=0, keepdims=True)
    grad_normed = grad_hidden * (1.0 + mod_ref[0:1, :])
    first_mean = jnp.mean(grad_normed, axis=-1, keepdims=True)
    second_mean = jnp.mean(grad_normed * normed, axis=-1, keepdims=True)
    mid_ref[...] = wide(dy_ref[...]) + scaling * (grad_normed - first_mean - normed * second_mean)
    span = weight_ref.shape[2]
    for columns in range(4):
        branch_ref[columns] = low(mid_ref[:, columns * span : (columns + 1) * span])
    for block, dest in enumerate(att_refs):
        at = pl.multiple_of(info[OWNER + block] * span, HEAD_DIM)
        total = dot_nt(branch_ref[0], weight_ref[0, pl.ds(at, span), :])
        for columns in range(1, 4):
            total = total + dot_nt(branch_ref[columns], weight_ref[columns, pl.ds(at, span), :])
        dest[...] = low(total)


def out_grad_kernel(info, branch_ref, *refs):
    near_ref, far_ref, att_ref = refs[4:]
    span = branch_ref.shape[2]
    natural(info, refs[:4], att_ref)
    for block in range(4):
        dest = near_ref if block < 2 else far_ref
        branch = branch_ref[info[OWNER + block]]
        for part in range(4):
            dest[block % 2, part * span : (part + 1) * span, :] = low(
                dot_tn(att_ref[part], branch)
            )


def attend_back_kernel(heads, rows, info, cos_ref, sin_ref, q_ref, k_ref, v_ref, *refs):
    att = refs[:4]
    grads = refs[4:8]
    out_ref, gx_ref, turn_ref, dq_ref, dk_ref, dv_ref = refs[8:]
    column = lax.broadcasted_iota(jnp.int32, (rows, HEAD_TILE), 1)

    def tile_of(ref, head):
        if head % 2 or head + 1 < heads:
            tile = wide(ref[:, HEAD_TILE * (head // 2) : HEAD_TILE * (head // 2) + HEAD_TILE])
            return pltpu.roll(tile, HEAD_DIM, 1) if head % 2 else tile
        last = wide(ref[:, head * HEAD_DIM :])
        return jnp.concatenate([last, jnp.zeros_like(last)], axis=1)

    for head in range(heads):
        there = slice(head * HEAD_TILE, (head + 1) * HEAD_TILE)
        for block in range(4):
            here = slice(block * rows, (block + 1) * rows)
            grad = jnp.where(column < HEAD_DIM, tile_of(grads[block], head), 0.0)
            minus = -jnp.sum(grad * tile_of(att[block], head), axis=-1, keepdims=True)
            first = wide(low(minus))
            gx_ref[here, :] = low(
                jnp.where(
                    column == HEAD_DIM,
                    first,
                    jnp.where(column == HEAD_DIM + 1, minus - first, grad),
                )
            )
        for block in range(4):
            here = slice(block * rows, (block + 1) * rows)
            keys = k_ref[here, there]
            probs = jnp.exp(dot_nt(keys, q_ref[:, there]))
            prob_grad = dot_nt(v_ref[here, there], gx_ref[...])
            score_grad = low(probs * prob_grad)
            dv_ref[here, there] = dot_nn(low(probs), gx_ref[...])
            dk_ref[here, there] = dot_nn(score_grad, q_ref[:, there])
            part = dot_tn(keys, score_grad)
            if block == 0:
                turn_ref[...] = part
            else:
                turn_ref[...] += part
        dq_ref[:, there] = jnp.transpose(turn_ref[...]) * 0.125

    for block in range(4):
        here = slice(block * rows, (block + 1) * rows)
        heads_of = [dq_ref[here, h * HEAD_TILE : (h + 1) * HEAD_TILE] for h in range(heads)]
        heads_of += [dk_ref[here, h * HEAD_TILE : (h + 1) * HEAD_TILE] for h in range(heads)]
        heads_of += [dv_ref[here, h * HEAD_TILE : (h + 1) * HEAD_TILE] for h in range(heads)]
        heads_of.append(jnp.zeros((rows, HEAD_TILE), jnp.float32))
        for tile in range((3 * heads + 1) // 2):
            both = jnp.where(
                column < HEAD_DIM,
                heads_of[2 * tile],
                pltpu.roll(heads_of[2 * tile + 1], HEAD_DIM, 1),
            )
            if tile < heads:
                both = both * cos_ref[here, :] - swap_halves(both) * sin_ref[here, :]
            out_ref[here, tile * HEAD_TILE : (tile + 1) * HEAD_TILE] = low(both)


def hidden_grad_kernel(info, grad_ref, weight_ref, near_ref, far_ref):
    rows = near_ref.shape[0] // 2
    span = grad_ref.shape[1]
    for block in (2, 3, 1, 0):
        dest = near_ref if block < 2 else far_ref
        at = (block % 2) * rows
        here = slice(block * rows, (block + 1) * rows)
        dest[at : at + rows, :] = low(dot_nt(grad_ref[here, :], weight_ref[:, :span]))


def qkv_grad_kernel(count, used, info, hidden_ref, grad_ref, near_ref, core_ref, chip_ref, *refs):
    outs, sums_ref = refs[:-1], refs[-1]
    total = dot_tn(hidden_ref[...], grad_ref[...])
    out_total = wide(near_ref[0]) + wide(core_ref[0]) + wide(chip_ref[0])
    per = total.shape[0] // count
    for index in range(count):
        here = slice(index * per, (index + 1) * per)
        sums_ref[index, :, :used] = low(total[here, :used])
        sums_ref[index, :, used:] = low(out_total[here, :])
    if len(outs) == 1:
        outs[0][...] = sums_ref[...]
    else:
        for index in range(count):
            outs[index][...] = sums_ref[info[PLACE + index]]


def input_kernel(info, gain, tok_ref, mid_ref, own_ref, core_ref, chip_ref, out_ref):
    rows = tok_ref.shape[0]
    grad_hidden = wide(own_ref[:rows, :]) + wide(core_ref[:rows, :]) + wide(chip_ref[...])
    normed, scaling = norm_rows(wide(tok_ref[...]))
    grad_normed = grad_hidden * gain[...]
    first_mean = jnp.mean(grad_normed, axis=-1, keepdims=True)
    second_mean = jnp.mean(grad_normed * normed, axis=-1, keepdims=True)
    out_ref[...] = low(
        mid_ref[...] + scaling * (grad_normed - first_mean - normed * second_mean)
    )


def finish_mlp_kernel(count, info, *refs):
    blocks = refs[:4]
    up_ref, down_ref, all_ref = refs[4:]
    natural(info, blocks, all_ref)
    rows = up_ref.shape[0]
    piece = down_ref.shape[0] // 4
    for part in range(4):
        value = wide(all_ref[part])
        for index in range(count):
            at = (index * 4 + part) * piece
            up_ref[:, at : at + piece] = value[:rows, index * piece : (index + 1) * piece]
        down_ref[part * piece : (part + 1) * piece, :] = value[rows:, :]


def finish_qkv_kernel(info, *refs):
    blocks = refs[:4]
    weight_ref, gain_ref, out_ref, own_ref, sums_ref, all_ref = refs[4:]
    natural(info, blocks, all_ref)
    span = all_ref.shape[2] // 4
    for part in range(4):
        value = wide(all_ref[part])
        for third in range(3):
            at = (third * 4 + part) * span
            out_ref[:, at : at + span] = value[:, third * span : (third + 1) * span]
        own_ref[:, part * span : (part + 1) * span] = value[:, 3 * span :]
    total = jnp.sum(wide(weight_ref[...]) * out_ref[...], axis=1, keepdims=True)
    wide_total = jnp.broadcast_to(total, (total.shape[0], HEAD_TILE))
    sums_ref[...] = jnp.transpose(wide_total)[0:1, :] / gain_ref[...]


def hop(values_in, mask):
    return lax.ppermute(values_in, "seq", [(i, i ^ mask) for i in range(lax.axis_size("seq"))])


def ring_of(count):
    return [0] + list(range(1, count, 2)) + [i for i in range(count - 1, 0, -1) if i % 2 == 0]


def ring_next(data_count):
    outer = data_count // 2
    ring = ring_of(outer)
    follow = {ring[i]: ring[(i + 1) % outer] for i in range(outer)}
    return [(z * 2 + y, follow[z] * 2 + y) for z in range(outer) for y in range(2)]


def ring_places(data_count, index):
    outer = data_count // 2
    ring = ring_of(outer)
    table = [[ring[(ring.index(z) - back) % outer] for z in range(outer)] for back in range(outer)]
    return [jnp.asarray(row, jnp.int32)[index // 2] for row in table]


def pair(values_in):
    return lax.ppermute(values_in, "dp", [(i, i ^ 1) for i in range(lax.axis_size("dp"))])


def dp_sum_direct(blocks):
    data_count = lax.axis_size("dp")
    if data_count != 8:
        return wide(lax.psum_scatter(blocks, "dp", scatter_dimension=0, tiled=False))
    return jnp.sum(wide(lax.all_to_all(blocks, "dp", 0, 0, tiled=True)), axis=0)


def after(values_in, *earlier):
    return lax.optimization_barrier((values_in,) + earlier)[0]


def onward(values_in):
    return lax.ppermute(values_in, "dp", ring_next(lax.axis_size("dp")))


def chunk_places():
    data_count = lax.axis_size("dp")
    if data_count != 8:
        return jnp.zeros((1,), jnp.int32)
    index = lax.axis_index("dp")
    ring = ring_of(data_count // 2)
    table = [
        [2 * ring[ring.index(one // 2) - back] + (one + side) % 2 for back in range(len(ring)) for side in (0, 1)]
        for one in range(data_count)
    ]
    return lax.dynamic_index_in_dim(jnp.asarray(table, jnp.int32), index, 0, keepdims=False)


def gathered_whole(chunk, sizes):
    gathered = lax.all_gather(chunk, "dp", axis=0)
    parts = []
    at = 0
    for size in sizes:
        parts.append(gathered[:, at : at + size].reshape(-1, chunk.shape[1]))
        at += size
    return [jnp.concatenate(parts, axis=0)]


def four(values_in):
    chip = hop(values_in, 2)
    return [values_in, chip, hop(values_in, 1), hop(chip, 1)]


def gather_back(near, far):
    rows = near.shape[0] // 2
    core = hop(far, 1)
    chip = hop(low(wide(near[rows:]) + wide(core[rows:])), 2)
    return core, chip


def body(tokens, ln1_gain, w_qkv, w_out, w_ada, w_up, w_down, out_grad, layout, timestep):
    seq_count = lax.axis_size("seq")
    data_count = lax.axis_size("dp")
    ringed = data_count == 8
    rank = lax.axis_index("seq")
    tok_rows, width = tokens.shape
    group_rows = tok_rows * seq_count
    heads_local = HEADS // seq_count
    local_width = heads_local * HEAD_DIM
    head_columns = heads_local * HEAD_TILE
    padded = (3 * heads_local + 1) // 2 * HEAD_TILE
    rows = w_qkv.shape[0]
    hidden = w_up.shape[1] // seq_count
    down_piece = w_down.shape[0] // seq_count
    rank_word = rank.reshape(1).astype(jnp.int32)

    tok_chip = hop(tokens, 2)
    first = run(
        first_part_kernel,
        [shaped((rows, 4 * local_width))],
        [rank_word, w_qkv, w_out],
        0,
        name="first_part",
    )[0]
    if ringed:
        held = [first, onward(first)]
        beside = [pair(first)]
        held[1], beside[0], tokens = lax.optimization_barrier((held[1], beside[0], tokens))
        held.append(onward(held[1]))
        beside.append(pair(held[1]))
        tok_core = hop(tokens, 1)
        held[2], beside[1], tok_chip, tok_core = lax.optimization_barrier(
            (held[2], beside[1], tok_chip, tok_core)
        )
        held.append(onward(held[2]))
        beside.append(pair(held[2]))
        tok_both = hop(tok_chip, 1)
    else:
        tok_core, tok_both = hop(tokens, 1), hop(tok_chip, 1)
    tok_blocks = [tokens, tok_chip, tok_core, tok_both]

    embed = low(time_table(wide(timestep), width))
    sent = jnp.stack(
        [embed.reshape(data_count, rows), jnp.broadcast_to(ln1_gain, (data_count, rows))], axis=1
    )
    taken = lax.all_to_all(sent, "dp", 0, 0, tiled=True)
    embeds = taken[:, 0]
    gain = wide(taken[:, 1].reshape(1, width))
    if ringed:
        embeds = after(embeds, held[1])
    mod_parts = jnp.dot(embeds, w_ada, preferred_element_type=jnp.float32)
    modulation = jnp.sum(lax.all_to_all(mod_parts, "dp", 0, 0, tiled=True), axis=0).reshape(
        3, width
    )

    masks = jnp.asarray(MASKS, jnp.int32)
    starts = (rank ^ masks) * tok_rows
    info = jnp.concatenate(
        [
            layout.reshape(-1),
            starts,
            rank ^ masks,
            masks[rank ^ jnp.arange(seq_count)],
            chunk_places(),
        ]
    )
    if ringed:
        starts = after(starts, held[2])
    positions = (starts[:, None] + jnp.arange(tok_rows, dtype=jnp.int32)[None, :]).reshape(-1)
    cos_table, sin_table = rope_tables(positions)

    second = run(
        functools.partial(second_part_kernel, data_count),
        [shaped((rows + down_piece, width))],
        [rank_word, w_up, w_down],
        0,
        name="second_part",
    )[0]
    if ringed:
        held[3], beside[2], second, *rest = lax.optimization_barrier(
            (held[3], beside[2], second, modulation, info, cos_table, sin_table, gain, tok_blocks)
        )
        modulation, info, cos_table, sin_table, gain, tok_blocks = rest
        beside.append(pair(held[3]))
        first_chunks = [part for both in zip(held, beside) for part in both]
        held = [second, onward(second)]
        grad_out, second = lax.optimization_barrier((out_grad, second, beside[3]))[:2]
        beside = [pair(second)]
        dy_chip = hop(grad_out, 2)
    else:
        first_chunks = gathered_whole(first, [rows])
        second_chunks = gathered_whole(second, [rows, down_piece])
        dy_chip = hop(out_grad, 2)
    count = len(first_chunks)
    up_rows = rows * (data_count // count)

    hidden_one, qkv_weight, own_out, queries, keys, values = run(
        functools.partial(qkv_kernel, heads_local, count),
        [
            shaped((group_rows, width)),
            shaped((width, 4 * local_width)),
            shaped((width, local_width)),
            shaped((group_rows, head_columns)),
            shaped((group_rows, head_columns)),
            shaped((group_rows, head_columns)),
        ],
        [info, gain, cos_table, sin_table] + tok_blocks + first_chunks,
        2 * group_rows * width * padded,
        name="qkv",
    )
    if ringed:
        queries, own_out, held[1], beside[0] = lax.optimization_barrier(
            (queries, own_out, held[1], beside[0])
        )
        beside.append(pair(held[1]))
        held.append(onward(held[1]))
    chip_out = hop(own_out, 2)
    *att_parts, marked = run(
        functools.partial(attend_kernel, heads_local, tok_rows),
        [shaped((tok_rows, local_width))] * 4 + [shaped((group_rows, head_columns))],
        [info, queries, keys, values],
        4 * group_rows * group_rows * head_columns,
        name="attend",
    )
    if ringed:
        att_parts, held[2], beside[1], chip_out, dy_chip = lax.optimization_barrier(
            (att_parts, held[2], beside[1], chip_out, dy_chip)
        )
        beside.append(pair(held[2]))
        held.append(onward(held[2]))
    att_own = [att_parts[0]] + [hop(att_parts[j], MASKS[j]) for j in (1, 2, 3)]
    if ringed:
        att_own, held[3], beside[2] = lax.optimization_barrier((att_own, held[3], beside[2]))
    out_blocks = [own_out, chip_out, hop(own_out, 1), hop(chip_out, 1)]
    middle, hidden_two = run(
        middle_kernel,
        [shaped((tok_rows, width), jnp.float32), shaped((tok_rows, width))],
        [info, tokens, modulation] + out_blocks + att_own,
        2 * tok_rows * width * width,
        scratch=[
            pltpu.VMEM((seq_count, tok_rows, local_width), jnp.bfloat16),
            pltpu.VMEM((seq_count, width, local_width), jnp.bfloat16),
        ],
        name="middle",
    )

    chip_hidden = hop(hidden_two, 2)
    if ringed:
        beside.append(pair(after(held[3], hidden_two)))
        second_chunks = [part for both in zip(held, beside) for part in both]
    hid_blocks = [hidden_two, chip_hidden, hop(hidden_two, 1), hop(chip_hidden, 1)]
    dy_blocks = [out_grad, dy_chip, hop(out_grad, 1), hop(dy_chip, 1)]
    grad_mlp, grad_act = run(
        functools.partial(act_grad_kernel, count, up_rows),
        [shaped((group_rows, width)), shaped((group_rows, hidden))],
        [info, modulation] + dy_blocks + second_chunks,
        2 * group_rows * width * hidden,
        scratch=[pltpu.VMEM((hidden, width), jnp.bfloat16)],
        name="act_grad",
    )
    half = shaped((group_rows // 2, width))
    activated, grad_pre, gh_near, gh_far = run(
        functools.partial(forward_kernel, count),
        [shaped((group_rows, hidden)), shaped((group_rows, hidden)), half, half],
        [info, grad_act] + hid_blocks + second_chunks,
        4 * group_rows * width * hidden,
        scratch=[pltpu.VMEM((width, hidden), jnp.bfloat16)],
        name="forward",
    )
    gh_core = hop(gh_far, 1)
    gh_send = low(wide(gh_near[tok_rows:]) + wide(gh_core[tok_rows:]))
    gh_chip = hop(gh_send, 2)
    block_shape = (rows + down_piece, width)
    grad_weights = run(
        functools.partial(weight_grad_kernel, data_count),
        [shaped(block_shape)] * count if ringed else [shaped((data_count,) + block_shape)],
        [info, after(activated, gh_send), grad_mlp, grad_pre] + hid_blocks,
        4 * group_rows * width * hidden,
        scratch=[pltpu.VMEM((data_count,) + block_shape, jnp.bfloat16)],
        name="weight_grad",
    )
    mlp_near, mlp_far, grad_gate = run(
        functools.partial(down_kernel, count, up_rows),
        [half, half, shaped((1, width), jnp.float32)],
        [info, after(activated, grad_weights[0])] + dy_blocks + second_chunks,
        2 * group_rows * width * hidden,
        scratch=[pltpu.VMEM((hidden, width), jnp.bfloat16)],
        name="down",
    )
    mlp_core = hop(mlp_far, 1)
    if ringed:
        grad_own, grad_other = list(grad_weights[0::2]), list(grad_weights[1::2])
        taken = pair(grad_other[1])

    grad_middle, branch, grad_sums, *grad_parts = run(
        branch_kernel,
        [
            shaped((tok_rows, width), jnp.float32),
            shaped((seq_count, tok_rows, local_width)),
            shaped((2, width), jnp.float32),
        ]
        + [shaped((tok_rows, local_width))] * 4,
        [info, modulation, after(middle, mlp_near), out_grad, gh_near, gh_core, gh_chip]
        + out_blocks,
        2 * tok_rows * width * width,
        scratch=[pltpu.VMEM((seq_count, width, local_width), jnp.bfloat16)],
        name="branch",
    )
    grad_parts, mlp_core = lax.optimization_barrier((grad_parts, mlp_core))
    grad_att = [grad_parts[0]] + [hop(grad_parts[j], MASKS[j]) for j in (1, 2, 3)]
    go_near, go_far = run(
        out_grad_kernel,
        [shaped((2, width, local_width))] * 2,
        [info, after(branch, grad_parts[0])] + att_own,
        2 * tok_rows * width * width,
        scratch=[pltpu.VMEM((seq_count, tok_rows, local_width), jnp.bfloat16)],
        name="out_grad",
    )
    go_core = hop(go_far, 1)
    go_send = low(wide(go_near[1:]) + wide(go_core[1:]))
    mlp_send = low(wide(mlp_near[tok_rows:]) + wide(mlp_core[tok_rows:]))

    grad_att, go_send, mlp_send = lax.optimization_barrier((grad_att, go_send, mlp_send))
    if ringed:
        ring_send = low(wide(after(grad_own[1], grad_parts[0])) + wide(taken))
        carried = onward(ring_send)
        taken = pair(after(grad_other[2], ring_send))
    go_chip = hop(go_send, 2)
    mlp_chip = hop(mlp_send, 2)
    grad_qkv = run(
        functools.partial(attend_back_kernel, heads_local, tok_rows),
        [shaped((group_rows, padded))],
        [info, cos_table, sin_table, marked, keys, values] + att_parts + grad_att,
        10 * group_rows * group_rows * head_columns,
        scratch=[
            pltpu.VMEM((group_rows, HEAD_TILE), jnp.bfloat16),
            pltpu.VMEM((HEAD_TILE, group_rows), jnp.float32),
            pltpu.VMEM((group_rows, head_columns), jnp.float32),
            pltpu.VMEM((group_rows, head_columns), jnp.float32),
            pltpu.VMEM((group_rows, head_columns), jnp.float32),
        ],
        name="attend_back",
    )[0]
    grad_qkv, go_chip = lax.optimization_barrier((grad_qkv, go_chip))
    qkv_sums = run(
        functools.partial(qkv_grad_kernel, data_count, 3 * local_width),
        [shaped((rows, 4 * local_width))] * count
        if ringed
        else [shaped((data_count, rows, 4 * local_width))],
        [info, hidden_one, grad_qkv, go_near, go_core, go_chip],
        2 * group_rows * width * padded,
        scratch=[pltpu.VMEM((data_count, rows, 4 * local_width), jnp.bfloat16)],
        name="qkv_grad",
    )
    if ringed:
        qkv_own, qkv_other = list(qkv_sums[0::2]), list(qkv_sums[1::2])
        qkv_taken = pair(qkv_other[1])
        mlp_ring = low(wide(after(grad_own[2], qkv_own[1])) + wide(taken) + wide(carried))
        carried = onward(mlp_ring)
        taken = pair(after(grad_other[3], mlp_ring))
    gq_near, gq_far = run(
        hidden_grad_kernel,
        [half, half],
        [info, after(grad_qkv, qkv_sums[0]), qkv_weight],
        2 * group_rows * width * padded,
        name="hidden_grad",
    )
    gq_core = hop(gq_far, 1)
    if ringed:
        qkv_ring = low(wide(after(qkv_own[1], gq_near)) + wide(qkv_taken))
        qkv_carried = onward(qkv_ring)
        qkv_taken = pair(after(qkv_other[2], qkv_ring))
    gq_send = low(wide(gq_near[tok_rows:]) + wide(gq_core[tok_rows:]))
    gq_send, mlp_chip = lax.optimization_barrier((gq_send, mlp_chip))
    gq_chip = hop(gq_send, 2)
    grad_mod = after(jnp.concatenate([grad_sums, grad_gate], axis=0), gq_send)
    grad_mod = grad_mod + hop(grad_mod, 1)
    mlp_out = wide(after(mlp_near[:tok_rows], gq_send)) + wide(mlp_core[:tok_rows]) + wide(mlp_chip)
    result = low(middle + modulation[2:3] * mlp_out)
    if ringed:
        qkv_carried, qkv_taken, carried, taken = lax.optimization_barrier(
            (qkv_carried, qkv_taken, carried, taken)
        )
        qkv_ring = low(wide(qkv_own[2]) + wide(qkv_taken) + wide(qkv_carried))
        qkv_carried = onward(qkv_ring)
        qkv_taken = pair(after(qkv_other[3], qkv_ring))
        mlp_ring = low(wide(after(grad_own[3], qkv_ring)) + wide(taken) + wide(carried))
        carried = onward(mlp_ring)
        taken = pair(after(grad_other[0], mlp_ring))
        qkv_carried, qkv_taken, gq_chip, grad_mod = lax.optimization_barrier(
            (qkv_carried, qkv_taken, gq_chip, grad_mod)
        )
        qkv_ring = low(wide(qkv_own[3]) + wide(qkv_taken) + wide(qkv_carried))
        qkv_carried = onward(qkv_ring)
        qkv_taken = pair(after(qkv_other[0], qkv_ring))
    grad_mod = grad_mod + hop(grad_mod, 2)
    grad_inputs = run(
        input_kernel,
        [shaped((tok_rows, width))],
        [info, gain, tokens, grad_middle, gq_near, gq_core, gq_chip],
        20 * tok_rows * width,
        name="input",
    )[0]
    if ringed:
        sum_mlp = low(wide(after(grad_own[0], qkv_ring)) + wide(taken) + wide(carried))
        sum_mlp, qkv_carried, qkv_taken, grad_inputs = lax.optimization_barrier(
            (sum_mlp, qkv_carried, qkv_taken, grad_inputs)
        )
        sum_qkv = low(wide(qkv_own[0]) + wide(qkv_taken) + wide(qkv_carried))
    else:
        sum_mlp = low(dp_sum_direct(grad_weights[0]))
        sum_qkv = low(dp_sum_direct(qkv_sums[0]))
    grad_mods = lax.all_to_all(
        jnp.broadcast_to(grad_mod[None], (data_count, 3, width)), "dp", 0, 0, tiled=True
    ).reshape(data_count, 3 * width)
    final_ada = lax.dot_general(
        wide(embeds), grad_mods, (((0,), (0,)), ((), ())), precision=lax.Precision.HIGHEST
    )

    final_up, final_down = run(
        functools.partial(finish_mlp_kernel, data_count),
        [shaped(w_up.shape, jnp.float32), shaped(w_down.shape, jnp.float32)],
        [info] + four(sum_mlp),
        0,
        scratch=[pltpu.VMEM((seq_count,) + block_shape, jnp.bfloat16)],
        name="finish_mlp",
    )
    final_qkv, final_out, final_gain = run(
        finish_qkv_kernel,
        [
            shaped(w_qkv.shape, jnp.float32),
            shaped(w_out.shape, jnp.float32),
            shaped((1, rows), jnp.float32),
        ],
        [info] + four(sum_qkv) + [w_qkv, wide(ln1_gain).reshape(1, rows)],
        0,
        scratch=[pltpu.VMEM((seq_count, rows, 4 * local_width), jnp.bfloat16)],
        name="finish_qkv",
    )
    return (
        result,
        grad_inputs,
        final_gain.reshape(-1),
        final_qkv,
        final_out,
        final_ada,
        final_up,
        final_down,
    )


def solution(mesh):
    placed = (
        P(("dp", "seq"), None),
        P("dp"),
        P("dp", None),
        P("dp", None),
        P("dp", None),
        P("dp", None),
        P("dp", None),
        P(("dp", "seq"), None),
        P("dp", None),
        P("dp"),
    )
    return jax.shard_map(
        body,
        mesh=mesh,
        in_specs=placed,
        out_specs=(
            P(("dp", "seq"), None),
            P(("dp", "seq"), None),
            P("dp"),
            P("dp", None),
            P("dp", None),
            P("dp", None),
            P("dp", None),
            P("dp", None),
        ),
        check_vma=False,
    )
```

time: 366 us -> 265 us (0.72); the launches traced: 360 us -> 263 us
  Pallas kernels: 0 us -> 94.6 us
  matrix products: 55.5 us -> 1.63 us
  starting transfers between devices: 103 us -> 61.3 us
  local copies, waits for them, and re-layouts: 54.2 us -> 15.3 us
  waiting for transfers between devices: 101 us -> 71.1 us
  other arithmetic: 40.4 us -> 17.2 us
    pallas_call x0 -> x17, Pallas kernels: none -> 94.6 us  [run(): return call(*args)]
    dot_general x17 -> x0, matrix products: 44 us -> none  [the longest x4 10.4 us: right_product(): lax.dot_general(left, right, (((1,), (1,)), ((), ())), preferred_element_...]
    ppermute x17 -> x12, waiting for transfers between devices: 28.4 us -> 8.25 us  [onward(): return lax.ppermute(values_in, 'dp', ring_next(lax.axis_size('dp')))]
    ppermute x17 -> x12, starting transfers between devices: 36.7 us -> 17.2 us  [onward(): return lax.ppermute(values_in, 'dp', ring_next(lax.axis_size('dp')))]
    dynamic_update_slice x24 -> x0, local copies, waits for them, and re-layouts: 13.5 us -> none  [the longest x12 7.99 us: dp_gather(): out = lax.dynamic_update_index_in_dim(out, held, own_row, 0)]
    all_to_all x2 -> x0, starting transfers between devices: 10.1 us -> none  [dp_sum_direct(): return jnp.sum(wide(lax.all_to_all(blocks, 'dp', 0, 0, tiled=True)), axis=0)]
    all_to_all x2 -> x0, waiting for transfers between devices: 9.82 us -> none  [dp_sum_direct(): return jnp.sum(wide(lax.all_to_all(blocks, 'dp', 0, 0, tiled=True)), axis=0)]
    sub x1 -> x0, matrix products: 8.82 us -> none  [body(): exponent = jnp.exp(scores - row_max)]
  transfers between devices with their start and end apart: 72 -> 65, of which waited for: 26 -> 17; matrix products, arithmetic and copies ran while one was open for 37% -> 10% of each run, Pallas kernels for 0% -> 25%
where the time goes in v2:
time: 265 us; the launch traced here: 263 us
  Pallas kernels  94.6 us (36%)
  waiting for transfers between devices  71.1 us (27%)
  starting transfers between devices  61.3 us (23%)
  other arithmetic  17.2 us (6%)
  local copies, waits for them, and re-layouts  15.3 us (6%)
    pallas_call x17, Pallas kernels, run(): return call(*args)  94.6 us
    ppermute x34, waiting for transfers between devices, hop(): lax.ppermute(values_in, 'seq', [(i, i ^ mask) for i in range(lax.axis_siz...  38.6 us
    ppermute x34, starting transfers between devices, hop(): lax.ppermute(values_in, 'seq', [(i, i ^ mask) for i in range(lax.axis_siz...  17.3 us
    ppermute x12, starting transfers between devices, onward(): return lax.ppermute(values_in, 'dp', ring_next(lax.axis_size('dp')))  17.2 us
    ppermute x16, starting transfers between devices, pair(): lax.ppermute(values_in, 'dp', [(i, i ^ 1) for i in range(lax.axis_size('d...  14.8 us
    ppermute x16, waiting for transfers between devices, pair(): lax.ppermute(values_in, 'dp', [(i, i ^ 1) for i in range(lax.axis_size('d...  13.4 us
    convert_element_type x13, other arithmetic, low(): return values_in.astype(jnp.bfloat16)  12.6 us
    ppermute x12, waiting for transfers between devices, onward(): return lax.ppermute(values_in, 'dp', ring_next(lax.axis_size('dp')))  8.25 us
  transfers between devices with their start and end apart: 65, of which 17 were waited for; matrix products, arithmetic and copies ran while one was open for 10% of the time, Pallas kernels for 25%

profile of v2, /device:TPU:0, one launch (start us, length us, event | category | flops | bytes accessed | tf_op | source)
XLA Modules:
  0.0 263.3 jit_solution(7772320071874427948)
XLA Ops:
  2.5 3.0 %collective-permute-start = (bf16[96,768]{1,0:T(8,128)(2,1)}, bf16[96,768]{1,0:T(8,128)(2,1)S(1)}, u32[]{:S(2)}, u32[]{:S(2)}) collective-permute-start(bf16[96,768]{1,0:T(8,128)(2,1)} %first_part.1.refs_7_), channel_id=1, source_target_pairs={{0,8},{4,12},{8,24},{12,28},{16,0},{20,4},{24,16},{28,20},{1,9},{5... | collective-permute-start | bytes 442376 | tf_op jit(solution)/shard_map/ppermute | solution.py:546
  10.7 3.9 %all-to-all-start = ((bf16[8,2,96]{2,1,0:T(2,128)(2,1)}), bf16[8,2,96]{2,1,0:T(2,128)(2,1)S(1)}, u32[]{:S(2)}, u32[]{:S(2)}) async-start(bf16[8,2,96]{2,1,0:T(2,128)(2,1)} %copy.24), calls=%async_computation | async-start | bytes 8192 | tf_op jit(solution)/shard_map/all_to_all | solution.py:629
  15.3 5.6 %all-to-all-done = bf16[8,2,96]{2,1,0:T(2,128)(2,1)S(1)} async-done(((bf16[8,2,96]{2,1,0:T(2,128)(2,1)}), bf16[8,2,96]{2,1,0:T(2,128)(2,1)S(1)}, u32[]{:S(2)}, u32[]{:S(2)}) %all-to-all-start) | async-done | bytes 3104 | tf_op jit(solution)/shard_map/all_to_all | solution.py:629
  22.9 4.5 %all-to-all-start.1 = ((f32[8,1,2304]{2,1,0:T(1,128)}), f32[8,1,2304]{2,1,0:T(1,128)S(1)}, u32[]{:S(2)}, u32[]{:S(2)}) async-start(f32[8,1,2304]{2,1,0:T(1,128)} %copy.26), calls=%async_computation.1 | async-start | bytes 147456 | tf_op jit(solution)/shard_map/all_to_all | solution.py:635
  32.2 2.3 all-to-all-done.1
  36.6 3.1 %fusion = (f32[1024,128]{1,0:T(8,128)}, f32[1024,128]{1,0:T(8,128)}) fusion(f32[128]{0:T(128)S(1)} %get-tuple-element.296, f32[128]{0:T(128)S(1)} %get-tuple-element.297, f32[1024]{0:T(1024)S(1)} %bitcast.31), kind=kLoop, calls=%fused_computation.13 | loop fusion | flops 262144 | bytes 1053696 | tf_op jit(solution)/shard_map/mul | solution.py:49
  41.7 2.3 collective-permute-start.10
  44.1 2.5 collective-permute-done.9.refs_14_
  47.6 6.6 %qkv.1 = (bf16[1024,768]{1,0:T(8,128)(2,1)}, bf16[768,768]{1,0:T(8,128)(2,1)}, bf16[768,192]{1,0:T(8,128)(2,1)}, bf16[1024,384]{1,0:T(8,128)(2,1)}, bf16[1024,38...) custom-call(s32[22]{0:T(128)} %concatenate.13.info, f32[1,768]{1,0:T(1,128)} %reshape.153.refs_0_.gain, ...), custom_call_target="tpu_custom_call" | custom-call | flops 6039797760 | bytes 55265808 | tf_op jit(solution)/shard_map/qkv/pallas_call | solution.py:105
  54.2 2.7 %collective-permute-start.12 = (bf16[192,768]{1,0:T(8,128)(2,1)S(1)}, bf16[192,768]{1,0:T(8,128)(2,1)S(1)}, u32[]{:S(2)}, u32[]{:S(2)}) collective-permute-start(bf16[192,768]{1,0:T(8,128)(2,1)S(1)} %collective-permute-done.10.refs_6_), channel_id=1, source_target_pairs={{0,8},{4,12},{8,24},{12,28},{16,0},{20,4},{24,16},{28,20},{1,9},{5... | collective-permute-start | bytes 884744 | tf_op jit(solution)/shard_map/ppermute | solution.py:546
  59.4 8.5 %attend.1 = (bf16[256,192]{1,0:T(8,128)(2,1)}, bf16[256,192]{1,0:T(8,128)(2,1)}, bf16[256,192]{1,0:T(8,128)(2,1)}, bf16[256,192]{1,0:T(8,128)(2,1)}, bf16[1024,384]{1,0:T(8,128)(2,1)}) custom-call(s32[22]{0:T(128)} %concatenate.13.info, bf16[1024,384]{1,0:T(8,128)(2,1)} %get-tuple-element.174.q_ref, bf16[1024,384]{1,0:T(8,128)(2,1)} %get-tuple-element.175.k_ref, ...), custom_call_target="tpu_custom_call" | custom-call | flops 9663676416 | bytes 21234192 | tf_op jit(solution)/shard_map/attend/pallas_call | solution.py:105
  75.2 5.3 %collective-permute-done.20.refs_7_.refs_3_ = bf16[256,192]{1,0:T(8,128)(2,1)S(1)} collective-permute-done((bf16[256,192]{1,0:T(8,128)(2,1)}, bf16[256,192]{1,0:T(8,128)(2,1)S(1)}, u32[]{:S(2)}, u32[]{:S(2)}) %collective-permute-start.20) | collective-permute-done | bytes 98336 | tf_op jit(solution)/shard_map/ppermute | solution.py:509
  82.8 3.6 %middle.1 = (f32[256,768]{1,0:T(8,128)}, bf16[256,768]{1,0:T(8,128)(2,1)}) custom-call(s32[22]{0:T(128)} %concatenate.13.info, bf16[256,768]{1,0:T(8,128)(2,1)} %tok_ref.1, f32[3,768]{1,0:T(4,128)} %reshape.147.mod_ref, bf16[768,192]{1,0:T(8,128)(2,1)} %get-tuple-element.173.refs_0_, bf16[768,192]{1,0:T(8,128)(2,1)} %copy-done.30, ...), custom_call_target="tpu_custom_call" | custom-call | flops 1811939328 | bytes 18930192 | tf_op jit(solution)/shard_map/middle/pallas_call | solution.py:105
  88.5 9.3 %collective-permute-done.26.refs_1_ = bf16[256,768]{1,0:T(8,128)(2,1)S(1)} collective-permute-done((bf16[256,768]{1,0:T(8,128)(2,1)}, bf16[256,768]{1,0:T(8,128)(2,1)S(1)}, u32[]{:S(2)}, u32[]{:S(2)}) %collective-permute-start.26) | collective-permute-done | bytes 393248 | tf_op jit(solution)/shard_map/ppermute | solution.py:509
  98.7 4.9 %act_grad.1 = (bf16[1024,768]{1,0:T(8,128)(2,1)}, bf16[1024,768]{1,0:T(8,128)(2,1)}) custom-call(s32[22]{0:T(128)} %concatenate.13.info, f32[3,768]{1,0:T(4,128)} %reshape.147.mod_ref, bf16[256,768]{1,0:T(8,128)(2,1)} %dy_ref.1, bf16[256,768]{1,0:T(8,128)(2,1)} %copy-done.29, bf16[256,768]{1,0:T(8,128)(2,1)} %copy-done.35, bf16[256,768]{1,0:T(8,128)(2,1)} %copy-done.36, ...), custom_call_target="tpu_custom_call" | custom-call | flops 7247757312 | bytes 42523152 | tf_op jit(solution)/shard_map/act_grad/pallas_call | solution.py:105
  104.5 8.0 %forward.1 = (bf16[1024,768]{1,0:T(8,128)(2,1)}, bf16[1024,768]{1,0:T(8,128)(2,1)}, bf16[512,768]{1,0:T(8,128)(2,1)}, bf16[512,768]{1,0:T(8,128)(2,1)}) custom-call(s32[22]{0:T(128)} %concatenate.13.info, bf16[1024,768]{1,0:T(8,128)(2,1)} %get-tuple-element.201.act_grad, bf16[256,768]{1,0:T(8,128)(2,1)} %get-tuple-element.199.refs_0_, ...), custom_call_target="tpu_custom_call" | custom-call | flops 14495514624 | bytes 61342224 | tf_op jit(solution)/shard_map/forward/pallas_call | solution.py:105
  116.5 6.8 %weight_grad.1 = (bf16[192,768]{1,0:T(8,128)(2,1)}, bf16[192,768]{1,0:T(8,128)(2,1)}, bf16[192,768]{1,0:T(8,128)(2,1)}, bf16[192,768]{1,0:T(8,128)(2,1)}, bf16[1...) custom-call(s32[22]{0:T(128)} %concatenate.13.info, ...), custom_call_target="tpu_custom_call" | custom-call | flops 14495514624 | bytes 51905040 | tf_op jit(solution)/shard_map/weight_grad/pallas_call | solution.py:105
  123.3 4.9 %down.1 = (bf16[512,768]{1,0:T(8,128)(2,1)}, bf16[512,768]{1,0:T(8,128)(2,1)}, f32[1,768]{1,0:T(1,128)}) custom-call(s32[22]{0:T(128)} %concatenate.13.info, bf16[1024,768]{1,0:T(8,128)(2,1)} %get-tuple-element.209.act_ref, bf16[256,768]{1,0:T(8,128)(2,1)} %dy_ref.1, bf16[256,768]{1,0:T(8,128)(2,1)} %copy-done.29, bf16[256,768]{1,0:T(8,128)(2,1)} %copy-done.35, ...), custom_call_target="tpu_custom_call" | custom-call | flops 7247757312 | bytes 42486288 | tf_op jit(solution)/shard_map/down/pallas_call | solution.py:105
  130.2 9.6 %collective-permute-done.30.chip_ref = bf16[256,768]{1,0:T(8,128)(2,1)S(1)} collective-permute-done((bf16[256,768]{1,0:T(8,128)(2,1)S(1)}, bf16[256,768]{1,0:T(8,128)(2,1)S(1)}, u32[]{:S(2)}, u32[]{:S(2)}) %collective-permute-start.30) | collective-permute-done | bytes 393248 | tf_op jit(solution)/shard_map/ppermute | solution.py:509
  140.5 14.6 %branch.1 = (f32[256,768]{1,0:T(8,128)}, bf16[4,256,192]{2,1,0:T(8,128)(2,1)}, f32[2,768]{1,0:T(2,128)}, bf16[256,192]{1,0:T(8,128)(2,1)}, bf16[256,192]{1,0:T(8...) custom-call(s32[22]{0:T(128)} %concatenate.13.info, f32[3,768]{1,0:T(4,128)} %reshape.147.mod_ref, ...), custom_call_target="tpu_custom_call" | custom-call | flops 1811939328 | bytes 35482128 | tf_op jit(solution)/shard_map/branch/pallas_call | solution.py:105
  155.2 3.0 %out_grad.1 = (bf16[2,768,192]{2,1,0:T(8,128)(2,1)}, bf16[2,768,192]{2,1,0:T(8,128)(2,1)}) custom-call(s32[22]{0:T(128)} %concatenate.13.info, bf16[4,256,192]{2,1,0:T(8,128)(2,1)} %get-tuple-element.223.branch_ref, bf16[256,192]{1,0:T(8,128)(2,1)} %get-tuple-element.189.refs_4_.refs_0_, bf16[256,192]{1,0:T(8,128)(2,1)} %copy-done.58, ...), custom_call_target="tpu_custom_call" | custom-call | flops 1811939328 | bytes 11797008 | tf_op jit(solution)/shard_map/out_grad/pallas_call | solution.py:105
  169.0 11.8 %attend_back.1.grad_ref = bf16[1024,640]{1,0:T(8,128)(2,1)} custom-call(s32[22]{0:T(128)} %concatenate.13.info, f32[1024,128]{1,0:T(8,128)} %get-tuple-element.159.refs_1_.cos_ref, f32[1024,128]{1,0:T(8,128)} %get-tuple-element.160.refs_2_.sin_ref, bf16[1024,384]{1,0:T(8,128)(2,1)} %get-tuple-element.211.q_ref, bf16[1024,384]{1,0:T(8,128)(2,1)} %get-tuple-element.175.k_ref, ...), custom_call_target="tpu_custom_call" | custom-call | flops 24159191040 | bytes 33030672 | tf_op jit(solution)/shard_map/attend_back/pallas_call | solution.py:105
  180.8 4.8 %qkv_grad.1 = (bf16[96,768]{1,0:T(8,128)(2,1)}, bf16[96,768]{1,0:T(8,128)(2,1)}, bf16[96,768]{1,0:T(8,128)(2,1)}, bf16[96,768]{1,0:T(8,128)(2,1)}, bf16[96,768]{...) custom-call(s32[22]{0:T(128)} %concatenate.13.info, ...), custom_call_target="tpu_custom_call" | custom-call | flops 6039797760 | bytes 33227280 | tf_op jit(solution)/shard_map/qkv_grad/pallas_call | solution.py:105
  185.6 4.0 %hidden_grad.1 = (bf16[512,768]{1,0:T(8,128)(2,1)}, bf16[512,768]{1,0:T(8,128)(2,1)}) custom-call(s32[22]{0:T(128)} %concatenate.13.info, bf16[1024,640]{1,0:T(8,128)(2,1)} %attend_back.1.grad_ref, bf16[768,768]{1,0:T(8,128)(2,1)} %get-tuple-element.237.weight_ref), custom_call_target="tpu_custom_call" | custom-call | flops 6039797760 | bytes 24379920 | tf_op jit(solution)/shard_map/hidden_grad/pallas_call | solution.py:105
  198.9 6.5 %collective-permute-done.40 = bf16[96,768]{1,0:T(8,128)(2,1)S(1)} collective-permute-done((bf16[96,768]{1,0:T(8,128)(2,1)S(1)}, bf16[96,768]{1,0:T(8,128)(2,1)S(1)}, u32[]{:S(2)}, u32[]{:S(2)}) %collective-permute-start.40) | collective-permute-done | bytes 147488 | tf_op jit(solution)/shard_map/ppermute | solution.py:546
  207.6 8.0 %collective-permute-done.38 = bf16[256,768]{1,0:T(8,128)(2,1)} collective-permute-done((bf16[256,768]{1,0:T(8,128)(2,1)S(1)}, bf16[256,768]{1,0:T(8,128)(2,1)}, u32[]{:S(2)}, u32[]{:S(2)}) %collective-permute-start.38) | collective-permute-done | bytes 393248 | tf_op jit(solution)/shard_map/ppermute | solution.py:509
  221.1 9.9 %collective-permute-done.48 = bf16[96,768]{1,0:T(8,128)(2,1)S(1)} collective-permute-done((bf16[96,768]{1,0:T(8,128)(2,1)S(1)}, bf16[96,768]{1,0:T(8,128)(2,1)S(1)}, u32[]{:S(2)}, u32[]{:S(2)}) %collective-permute-start.48) | collective-permute-done | bytes 147488 | tf_op jit(solution)/shard_map/ppermute | solution.py:531
  235.6 3.2 %input.1 = bf16[256,768]{1,0:T(8,128)(2,1)} custom-call(s32[22]{0:T(128)} %concatenate.13.info, f32[1,768]{1,0:T(1,128)} %reshape.153.refs_0_.gain, bf16[256,768]{1,0:T(8,128)(2,1)} %tok_ref.1, f32[256,768]{1,0:T(8,128)} %get-tuple-element.278.mid_ref, bf16[512,768]{1,0:T(8,128)(2,1)} %get-tuple-element.238.own_ref, bf16[512,768]{1,0:T(8,128)(2,1)} %copy-done.4, ...), custom_call_target="tpu_custom_call" | custom-call | flops 23592960 | bytes 21252624 | tf_op jit(solution)/shard_map/input/pallas_call | solution.py:105
  242.5 3.7 %all-to-all-start.2 = ((f32[8,3,768]{2,1,0:T(4,128)}), f32[8,3,768]{2,1,0:T(4,128)S(1)}, u32[]{:S(2)}, u32[]{:S(2)}) async-start(f32[8,3,768]{2,1,0:T(4,128)} %broadcast_in_dim.12), calls=%async_computation.2 | async-start | bytes 196608 | tf_op jit(solution)/shard_map/all_to_all | solution.py:896
  250.4 2.9 %all-to-all-done.2 = f32[8,3,768]{2,1,0:T(4,128)S(1)} async-done(((f32[8,3,768]{2,1,0:T(4,128)}), f32[8,3,768]{2,1,0:T(4,128)S(1)}, u32[]{:S(2)}, u32[]{:S(2)}) %all-to-all-start.2) | async-done | bytes 73760 | tf_op jit(solution)/shard_map/all_to_all | solution.py:896
  256.7 2.6 finish_qkv.1
  260.0 3.1 %finish_mlp.1 = (f32[96,3072]{1,0:T(8,128)}, f32[384,768]{1,0:T(8,128)}) custom-call(s32[22]{0:T(128)} %concatenate.13.info, bf16[192,768]{1,0:T(8,128)(2,1)} %copy-done.5, bf16[192,768]{1,0:T(8,128)(2,1)} %collective-permute-done.59.refs_1_, bf16[192,768]{1,0:T(8,128)(2,1)} %copy-done.15, bf16[192,768]{1,0:T(8,128)(2,1)} %collective-permute-done.61.refs_3_), custom_call_target="tpu_custom_call" | custom-call | bytes 21234192 | tf_op jit(solution)/shard_map/finish_mlp/pallas_call | solution.py:105
  (284 shorter events, 85.2 us)
Async XLA Ops:
  2.5 12.7 %collective-permute-start = (bf16[96,768]{1,0:T(8,128)(2,1)}, bf16[96,768]{1,0:T(8,128)(2,1)S(1)}, u32[]{:S(2)}, u32[]{:S(2)}) collective-permute-start(bf16[96,768]{1,0:T(8,128)(2,1)} %first_part.1.refs_7_), channel_id=1, source_target_pairs={{0,8},{4,12},{8,24},{12,28},{16,0},{20,4},{24,16},{28,20},{1,9},{5... | collective-permute-start | bytes 442376 | tf_op jit(solution)/shard_map/ppermute | solution.py:546
  7.1 28.2 %collective-permute-start.4 = (bf16[256,768]{1,0:T(8,128)(2,1)}, bf16[256,768]{1,0:T(8,128)(2,1)S(1)}, u32[]{:S(2)}, u32[]{:S(2)}) collective-permute-start(bf16[256,768]{1,0:T(8,128)(2,1)} %tok_ref.1), channel_id=1, source_target_pairs={{0,2},{1,3},{2,0},{3,1},{4,6},{5,7},{6,4},{7,5},{8,10},{9,11},{10,... | collective-permute-start | bytes 1179656 | tf_op jit(solution)/shard_map/ppermute | solution.py:509
  15.2 20.0 %collective-permute-start.5 = (bf16[256,768]{1,0:T(8,128)(2,1)}, bf16[256,768]{1,0:T(8,128)(2,1)S(1)}, u32[]{:S(2)}, u32[]{:S(2)}) collective-permute-start(bf16[256,768]{1,0:T(8,128)(2,1)} %tok_ref.1), channel_id=1, source_target_pairs={{0,1},{1,0},{2,3},{3,2},{4,5},{5,4},{6,7},{7,6},{8,9},{9,8},{10,11... | collective-permute-start | bytes 1179656 | tf_op jit(solution)/shard_map/ppermute | solution.py:509
  20.9 14.3 %collective-permute-start.2 = (bf16[96,768]{1,0:T(8,128)(2,1)S(1)}, bf16[96,768]{1,0:T(8,128)(2,1)S(1)}, u32[]{:S(2)}, u32[]{:S(2)}) collective-permute-start(bf16[96,768]{1,0:T(8,128)(2,1)S(1)} %collective-permute-done.refs_9_), channel_id=1, source_target_pairs={{0,8},{4,12},{8,24},{12,28},{16,0},{20,4},{24,16},{28,20},{1,9},{5... | collective-permute-start | bytes 442376 | tf_op jit(solution)/shard_map/ppermute | solution.py:546
  21.5 13.8 %collective-permute-start.3 = (bf16[96,768]{1,0:T(8,128)(2,1)S(1)}, bf16[96,768]{1,0:T(8,128)(2,1)S(1)}, u32[]{:S(2)}, u32[]{:S(2)}) collective-permute-start(bf16[96,768]{1,0:T(8,128)(2,1)S(1)} %collective-permute-done.refs_9_), channel_id=1, source_target_pairs={{0,4},{4,0},{8,12},{12,8},{16,20},{20,16},{24,28},{28,24},{1,5},{5... | collective-permute-start | bytes 442376 | tf_op jit(solution)/shard_map/ppermute | solution.py:531
  22.9 11.6 %all-to-all-start.1 = ((f32[8,1,2304]{2,1,0:T(1,128)}), f32[8,1,2304]{2,1,0:T(1,128)S(1)}, u32[]{:S(2)}, u32[]{:S(2)}) async-start(f32[8,1,2304]{2,1,0:T(1,128)} %copy.26), calls=%async_computation.1 | async-start | bytes 147456 | tf_op jit(solution)/shard_map/all_to_all | solution.py:635
  41.7 12.5 %collective-permute-start.10 = (bf16[192,768]{1,0:T(8,128)(2,1)}, bf16[192,768]{1,0:T(8,128)(2,1)S(1)}, u32[]{:S(2)}, u32[]{:S(2)}) collective-permute-start(bf16[192,768]{1,0:T(8,128)(2,1)} %second_part.1.refs_4_), channel_id=1, source_target_pairs={{0,8},{4,12},{8,24},{12,28},{16,0},{20,4},{24,16},{28,20},{1,9},{5... | collective-permute-start | bytes 884744 | tf_op jit(solution)/shard_map/ppermute | solution.py:546
  47.0 21.0 %collective-permute-start.15 = (bf16[256,768]{1,0:T(8,128)(2,1)S(1)}, bf16[256,768]{1,0:T(8,128)(2,1)S(1)}, u32[]{:S(2)}, u32[]{:S(2)}) collective-permute-start(bf16[256,768]{1,0:T(8,128)(2,1)S(1)} %copy-done.27), channel_id=1, source_target_pairs={{0,2},{1,3},{2,0},{3,1},{4,6},{5,7},{6,4},{7,5},{8,10},{9,11},{10,... | collective-permute-start | bytes 1179656 | tf_op jit(solution)/shard_map/ppermute | solution.py:509
  54.2 13.7 %collective-permute-start.12 = (bf16[192,768]{1,0:T(8,128)(2,1)S(1)}, bf16[192,768]{1,0:T(8,128)(2,1)S(1)}, u32[]{:S(2)}, u32[]{:S(2)}) collective-permute-start(bf16[192,768]{1,0:T(8,128)(2,1)S(1)} %collective-permute-done.10.refs_6_), channel_id=1, source_target_pairs={{0,8},{4,12},{8,24},{12,28},{16,0},{20,4},{24,16},{28,20},{1,9},{5... | collective-permute-start | bytes 884744 | tf_op jit(solution)/shard_map/ppermute | solution.py:546
  56.9 11.1 %collective-permute-start.13 = (bf16[192,768]{1,0:T(8,128)(2,1)S(1)}, bf16[192,768]{1,0:T(8,128)(2,1)S(1)}, u32[]{:S(2)}, u32[]{:S(2)}) collective-permute-start(bf16[192,768]{1,0:T(8,128)(2,1)S(1)} %collective-permute-done.10.refs_6_), channel_id=1, source_target_pairs={{0,4},{4,0},{8,12},{12,8},{16,20},{20,16},{24,28},{28,24},{1,5},{5... | collective-permute-start | bytes 884744 | tf_op jit(solution)/shard_map/ppermute | solution.py:531
  68.7 11.8 %collective-permute-start.21 = (bf16[192,768]{1,0:T(8,128)(2,1)S(1)}, bf16[192,768]{1,0:T(8,128)(2,1)S(1)}, u32[]{:S(2)}, u32[]{:S(2)}) collective-permute-start(bf16[192,768]{1,0:T(8,128)(2,1)S(1)} %collective-permute-done.12.refs_8_), channel_id=1, source_target_pairs={{0,8},{4,12},{8,24},{12,28},{16,0},{20,4},{24,16},{28,20},{1,9},{5... | collective-permute-start | bytes 884744 | tf_op jit(solution)/shard_map/ppermute | solution.py:546
  69.5 11.0 %collective-permute-start.22 = (bf16[192,768]{1,0:T(8,128)(2,1)S(1)}, bf16[192,768]{1,0:T(8,128)(2,1)S(1)}, u32[]{:S(2)}, u32[]{:S(2)}) collective-permute-start(bf16[192,768]{1,0:T(8,128)(2,1)S(1)} %collective-permute-done.12.refs_8_), channel_id=1, source_target_pairs={{0,4},{4,0},{8,12},{12,8},{16,20},{20,16},{24,28},{28,24},{1,5},{5... | collective-permute-start | bytes 884744 | tf_op jit(solution)/shard_map/ppermute | solution.py:531
  86.4 11.4 %collective-permute-start.26 = (bf16[256,768]{1,0:T(8,128)(2,1)}, bf16[256,768]{1,0:T(8,128)(2,1)S(1)}, u32[]{:S(2)}, u32[]{:S(2)}) collective-permute-start(bf16[256,768]{1,0:T(8,128)(2,1)} %get-tuple-element.199.refs_0_), channel_id=1, source_target_pairs={{0,2},{1,3},{2,0},{3,1},{4,6},{5,7},{6,4},{7,5},{8,10},{9,11},{10,... | collective-permute-start | bytes 1179656 | tf_op jit(solution)/shard_map/ppermute | solution.py:509
  87.0 10.8 %collective-permute-start.24 = (bf16[256,768]{1,0:T(8,128)(2,1)S(1)}, bf16[256,768]{1,0:T(8,128)(2,1)S(1)}, u32[]{:S(2)}, u32[]{:S(2)}) collective-permute-start(bf16[256,768]{1,0:T(8,128)(2,1)S(1)} %collective-permute-done.15.refs_1_), channel_id=1, source_target_pairs={{0,1},{1,0},{2,3},{3,2},{4,5},{5,4},{6,7},{7,6},{8,9},{9,8},{10,11... | collective-permute-start | bytes 1179656 | tf_op jit(solution)/shard_map/ppermute | solution.py:509
  88.5 15.1 %collective-permute-start.27 = (bf16[256,768]{1,0:T(8,128)(2,1)}, bf16[256,768]{1,0:T(8,128)(2,1)S(1)}, u32[]{:S(2)}, u32[]{:S(2)}) collective-permute-start(bf16[256,768]{1,0:T(8,128)(2,1)} %get-tuple-element.199.refs_0_), channel_id=1, source_target_pairs={{0,1},{1,0},{2,3},{3,2},{4,5},{5,4},{6,7},{7,6},{8,9},{9,8},{10,11... | collective-permute-start | bytes 1179656 | tf_op jit(solution)/shard_map/ppermute | solution.py:509
  128.2 26.9 %collective-permute-start.31 = (bf16[512,768]{1,0:T(8,128)(2,1)}, bf16[512,768]{1,0:T(8,128)(2,1)S(1)}, u32[]{:S(2)}, u32[]{:S(2)}) collective-permute-start(bf16[512,768]{1,0:T(8,128)(2,1)} %get-tuple-element.217), channel_id=1, source_target_pairs={{0,1},{1,0},{2,3},{3,2},{4,5},{5,4},{6,7},{7,6},{8,9},{9,8},{10,11... | collective-permute-start | bytes 2359304 | tf_op jit(solution)/shard_map/ppermute | solution.py:509
  128.6 11.2 %collective-permute-start.30 = (bf16[256,768]{1,0:T(8,128)(2,1)S(1)}, bf16[256,768]{1,0:T(8,128)(2,1)S(1)}, u32[]{:S(2)}, u32[]{:S(2)}) collective-permute-start(bf16[256,768]{1,0:T(8,128)(2,1)S(1)} %add_convert_fusion.4), channel_id=1, source_target_pairs={{0,2},{1,3},{2,0},{3,1},{4,6},{5,7},{6,4},{7,5},{8,10},{9,11},{10,... | collective-permute-start | bytes 1179656 | tf_op jit(solution)/shard_map/ppermute | solution.py:509
  129.2 32.7 %collective-permute-start.42 = (bf16[192,768]{1,0:T(8,128)(2,1)}, bf16[192,768]{1,0:T(8,128)(2,1)}, u32[]{:S(2)}, u32[]{:S(2)}) collective-permute-start(bf16[192,768]{1,0:T(8,128)(2,1)} %get-tuple-element.256), channel_id=1, source_target_pairs={{0,4},{4,0},{8,12},{12,8},{16,20},{20,16},{24,28},{28,24},{1,5},{5... | collective-permute-start | bytes 884744 | tf_op jit(solution)/shard_map/ppermute | solution.py:531
  163.7 27.3 %collective-permute-start.44 = (bf16[192,768]{1,0:T(8,128)(2,1)}, bf16[192,768]{1,0:T(8,128)(2,1)}, u32[]{:S(2)}, u32[]{:S(2)}) collective-permute-start(bf16[192,768]{1,0:T(8,128)(2,1)} %add_convert_fusion.8), channel_id=1, source_target_pairs={{0,8},{4,12},{8,24},{12,28},{16,0},{20,4},{24,16},{28,20},{1,9},{5... | collective-permute-start | bytes 884744 | tf_op jit(solution)/shard_map/ppermute | solution.py:546
  165.3 25.8 %collective-permute-start.43 = (bf16[192,768]{1,0:T(8,128)(2,1)}, bf16[192,768]{1,0:T(8,128)(2,1)}, u32[]{:S(2)}, u32[]{:S(2)}) collective-permute-start(bf16[192,768]{1,0:T(8,128)(2,1)} %get-tuple-element.257), channel_id=1, source_target_pairs={{0,4},{4,0},{8,12},{12,8},{16,20},{20,16},{24,28},{28,24},{1,5},{5... | collective-permute-start | bytes 884744 | tf_op jit(solution)/shard_map/ppermute | solution.py:531
  168.3 12.5 %collective-permute-start.36 = (bf16[1,768,192]{2,1,0:T(8,128)(2,1)S(1)}, bf16[1,768,192]{2,1,0:T(8,128)(2,1)}, u32[]{:S(2)}, u32[]{:S(2)}) collective-permute-start(bf16[1,768,192]{2,1,0:T(8,128)(2,1)S(1)} %add_convert_fusion.3), channel_id=1, source_target_pairs={{0,2},{1,3},{2,0},{3,1},{4,6},{5,7},{6,4},{7,5},{8,10},{9,11},{10,... | collective-permute-start | bytes 884744 | tf_op jit(solution)/shard_map/ppermute | solution.py:509
  189.7 17.7 %collective-permute-start.37 = (bf16[512,768]{1,0:T(8,128)(2,1)}, bf16[512,768]{1,0:T(8,128)(2,1)S(1)}, u32[]{:S(2)}, u32[]{:S(2)}) collective-permute-start(bf16[512,768]{1,0:T(8,128)(2,1)} %get-tuple-element.239), channel_id=1, source_target_pairs={{0,1},{1,0},{2,3},{3,2},{4,5},{5,4},{6,7},{7,6},{8,9},{9,8},{10,11... | collective-permute-start | bytes 2359304 | tf_op jit(solution)/shard_map/ppermute | solution.py:509
  192.2 14.4 %collective-permute-start.45 = (bf16[192,768]{1,0:T(8,128)(2,1)S(1)}, bf16[192,768]{1,0:T(8,128)(2,1)S(1)}, u32[]{:S(2)}, u32[]{:S(2)}) collective-permute-start(bf16[192,768]{1,0:T(8,128)(2,1)S(1)} %add_convert_fusion.7), channel_id=1, source_target_pairs={{0,8},{4,12},{8,24},{12,28},{16,0},{20,4},{24,16},{28,20},{1,9},{5... | collective-permute-start | bytes 884744 | tf_op jit(solution)/shard_map/ppermute | solution.py:546
  194.1 12.6 %collective-permute-start.46 = (bf16[192,768]{1,0:T(8,128)(2,1)}, bf16[192,768]{1,0:T(8,128)(2,1)S(1)}, u32[]{:S(2)}, u32[]{:S(2)}) collective-permute-start(bf16[192,768]{1,0:T(8,128)(2,1)} %get-tuple-element.259), channel_id=1, source_target_pairs={{0,4},{4,0},{8,12},{12,8},{16,20},{20,16},{24,28},{28,24},{1,5},{5... | collective-permute-start | bytes 884744 | tf_op jit(solution)/shard_map/ppermute | solution.py:531
  206.8 14.3 %collective-permute-start.47 = (bf16[96,768]{1,0:T(8,128)(2,1)S(1)}, bf16[96,768]{1,0:T(8,128)(2,1)S(1)}, u32[]{:S(2)}, u32[]{:S(2)}) collective-permute-start(bf16[96,768]{1,0:T(8,128)(2,1)S(1)} %add_convert_fusion.11), channel_id=1, source_target_pairs={{0,8},{4,12},{8,24},{12,28},{16,0},{20,4},{24,16},{28,20},{1,9},{5... | collective-permute-start | bytes 442376 | tf_op jit(solution)/shard_map/ppermute | solution.py:546
  215.6 15.4 %collective-permute-start.49 = (bf16[256,768]{1,0:T(8,128)(2,1)S(1)}, bf16[256,768]{1,0:T(8,128)(2,1)S(1)}, u32[]{:S(2)}, u32[]{:S(2)}) collective-permute-start(bf16[256,768]{1,0:T(8,128)(2,1)S(1)} %add_convert_fusion.1), channel_id=1, source_target_pairs={{0,2},{1,3},{2,0},{3,1},{4,6},{5,7},{6,4},{7,5},{8,10},{9,11},{10,... | collective-permute-start | bytes 1179656 | tf_op jit(solution)/shard_map/ppermute | solution.py:509
  217.7 21.1 %collective-permute-start.52 = (bf16[192,768]{1,0:T(8,128)(2,1)}, bf16[192,768]{1,0:T(8,128)(2,1)}, u32[]{:S(2)}, u32[]{:S(2)}) collective-permute-start(bf16[192,768]{1,0:T(8,128)(2,1)} %add_convert_fusion.6), channel_id=1, source_target_pairs={{0,8},{4,12},{8,24},{12,28},{16,0},{20,4},{24,16},{28,20},{1,9},{5... | collective-permute-start | bytes 884744 | tf_op jit(solution)/shard_map/ppermute | solution.py:546
  218.5 20.3 %collective-permute-start.51 = (bf16[192,768]{1,0:T(8,128)(2,1)}, bf16[192,768]{1,0:T(8,128)(2,1)}, u32[]{:S(2)}, u32[]{:S(2)}) collective-permute-start(bf16[192,768]{1,0:T(8,128)(2,1)} %get-tuple-element.275), channel_id=1, source_target_pairs={{0,4},{4,0},{8,12},{12,8},{16,20},{20,16},{24,28},{28,24},{1,5},{5... | collective-permute-start | bytes 884744 | tf_op jit(solution)/shard_map/ppermute | solution.py:531
  219.7 11.3 %collective-permute-start.48 = (bf16[96,768]{1,0:T(8,128)(2,1)S(1)}, bf16[96,768]{1,0:T(8,128)(2,1)S(1)}, u32[]{:S(2)}, u32[]{:S(2)}) collective-permute-start(bf16[96,768]{1,0:T(8,128)(2,1)S(1)} %copy-done.50), channel_id=1, source_target_pairs={{0,4},{4,0},{8,12},{12,8},{16,20},{20,16},{24,28},{28,24},{1,5},{5... | collective-permute-start | bytes 442376 | tf_op jit(solution)/shard_map/ppermute | solution.py:531
  242.5 10.8 %all-to-all-start.2 = ((f32[8,3,768]{2,1,0:T(4,128)}), f32[8,3,768]{2,1,0:T(4,128)S(1)}, u32[]{:S(2)}, u32[]{:S(2)}) async-start(f32[8,3,768]{2,1,0:T(4,128)} %broadcast_in_dim.12), calls=%async_computation.2 | async-start | bytes 196608 | tf_op jit(solution)/shard_map/all_to_all | solution.py:896
  246.2 13.1 %collective-permute-start.60 = (bf16[192,768]{1,0:T(8,128)(2,1)S(1)}, bf16[192,768]{1,0:T(8,128)(2,1)S(1)}, u32[]{:S(2)}, u32[]{:S(2)}) collective-permute-start(bf16[192,768]{1,0:T(8,128)(2,1)S(1)} %add_convert_fusion.5.refs_0_), channel_id=1, source_target_pairs={{0,1},{1,0},{2,3},{3,2},{4,5},{5,4},{6,7},{7,6},{8,9},{9,8},{10,11... | collective-permute-start | bytes 884744 | tf_op jit(solution)/shard_map/ppermute | solution.py:509
  248.3 11.0 %collective-permute-start.61 = (bf16[192,768]{1,0:T(8,128)(2,1)}, bf16[192,768]{1,0:T(8,128)(2,1)}, u32[]{:S(2)}, u32[]{:S(2)}) collective-permute-start(bf16[192,768]{1,0:T(8,128)(2,1)} %collective-permute-done.59.refs_1_), channel_id=1, source_target_pairs={{0,1},{1,0},{2,3},{3,2},{4,5},{5,4},{6,7},{7,6},{8,9},{9,8},{10,11... | collective-permute-start | bytes 884744 | tf_op jit(solution)/shard_map/ppermute | solution.py:509
  (94 other events, 877.0 us)
